TPU v7x, 256 devices: a whole 4x4x8 slice. The times are simulated.
256 devices in a mesh: frame: 32 (over x, z), space: 8 (over y, core).
Axes of the slice: x: 4, y: 4, z: 8, core: 2. Of those that a mesh axis runs over, the one named last changes fastest.
Arguments:
- queries: bfloat16 [128, 1024, 2240], P('frame', 'space'), may hold values from -6 to 6
- keys: bfloat16 [128, 1024, 2240], P('frame', 'space'), may hold values from -16 to 16
- values: bfloat16 [128, 1024, 2240], P('frame', 'space'), may hold values from -16 to 16
- out_weight: bfloat16 [2240, 2240], P('frame'), may hold values from -0.125 to 0.125
- conv_taps: float32 [3, 2240], replicated, may hold values from -3 to 3
Outputs:
- mixed: bfloat16 [128, 1024, 2240], P('frame', 'space')
All inputs are finite; a program needn't handle non-finite values.
Results may differ from a plain program's by a relative error of at most 0.0059.
Values may be sent and summed in bfloat16 or wider, within the bound.
No kernel may reach another device: no remote copies, remote signals or barrier semaphores. Data moves between devices by JAX's collectives and lax.ppermute only.
A program may use at most 192 MiB of HBM per device.

v0:
```python
import functools

import jax
import jax.numpy as jnp
from jax import lax
from jax.experimental import pallas as pl
from jax.experimental.pallas import tpu as pltpu
from jax.sharding import Mesh, PartitionSpec as P


HEADS = 20
HEAD_DIM = 112
D = HEADS * HEAD_DIM
LANES = 128
HALF_HEADS = HEADS // 2
HALF_ROWS = 1152
BLOCK, PADDED = 70, 72
PAIR = 2 * PADDED
CHUNK = 288
HALF_COLS = 1152
COL_TILE = 384

stab_eps = 1e-06


def shift(value, axis, distance, size):
    return lax.ppermute(value, axis, [(i, (i + distance) % size) for i in range(size)])


def next_section(value, size):
    return lax.ppermute(value, ("x", "z"), [(i, i + 1) for i in range(size - 1)])


def after(value, *others):
    return lax.optimization_barrier((value,) + others)[0]


def kv_kernel(core_ref, k_ref, v_ref, mine_ref, theirs_ref, acc_ref):
    frame = pl.program_id(0)
    core = core_ref[0]

    @pl.when(frame == 0)
    def _():
        acc_ref[...] = jnp.zeros_like(acc_ref)

    tokens = k_ref.shape[2]
    pad = jnp.zeros((LANES - HEAD_DIM, tokens), jnp.bfloat16)
    ones = (lax.broadcasted_iota(jnp.int32, (LANES, tokens), 0) == HEAD_DIM).astype(jnp.bfloat16)
    for head in range(HEADS):
        half, inner = divmod(head, HALF_HEADS)
        keys = jnp.maximum(k_ref[0, head * HEAD_DIM : (head + 1) * HEAD_DIM, :], 0)
        vals = v_ref[0, head * HEAD_DIM : (head + 1) * HEAD_DIM, :]
        left = jnp.concatenate([vals, keys], axis=1)
        right = jnp.concatenate([jnp.concatenate([keys, pad], axis=0), ones], axis=1)
        part = lax.dot_general(
            left, right, (((1,), (1,)), ((), ())), preferred_element_type=jnp.float32
        )
        rows = slice(inner * HEAD_DIM, (inner + 1) * HEAD_DIM)
        acc_ref[half, rows, :] = acc_ref[half, rows, :] + part
    norm = lax.broadcasted_iota(jnp.int32, (PADDED, LANES), 1) == HEAD_DIM
    for ref, half in ((mine_ref, core), (theirs_ref, 1 - core)):
        for pair in range(HALF_ROWS // PAIR):
            cuts = [
                jnp.where(norm, acc_ref[half, b * PADDED : (b + 1) * PADDED, :], acc_ref[half, b * BLOCK : b * BLOCK + PADDED, :])
                for b in (2 * pair, 2 * pair + 1)
            ]
            ref[0, pair * PAIR : (pair + 1) * PAIR, :] = jnp.concatenate(cuts, axis=0).astype(ref.dtype)


def limit(mib):
    return pltpu.CompilerParams(vmem_limit_bytes=mib << 20)


def local_kv(core, keys, values):
    frames, _, tokens = keys.shape
    spec = pl.BlockSpec((1, D, tokens), lambda f, c: (f, 0, 0))
    out = pl.BlockSpec((1, HALF_ROWS, LANES), lambda f, c: (f, 0, 0))
    return pl.pallas_call(
        kv_kernel,
        out_shape=[jax.ShapeDtypeStruct((frames, HALF_ROWS, LANES), jnp.bfloat16)] * 2,
        grid_spec=pltpu.PrefetchScalarGridSpec(
            num_scalar_prefetch=1,
            grid=(frames,),
            in_specs=[spec, spec],
            out_specs=[out, out],
            scratch_shapes=[pltpu.VMEM((2, HALF_ROWS, LANES), jnp.float32)],
        ),
        compiler_params=limit(60),
        cost_estimate=pl.CostEstimate(
            flops=4 * frames * tokens * D * LANES, bytes_accessed=4 * frames * tokens * D * 2, transcendentals=0
        ),
        name="local_kv",
    )(core, keys, values)


def copy_kernel(in_ref, out_ref):
    out_ref[...] = in_ref[...]


def last_two(queries):
    frames, _, tokens = queries.shape
    return pl.pallas_call(
        copy_kernel,
        out_shape=jax.ShapeDtypeStruct((2, D, tokens), queries.dtype),
        grid=(4,),
        in_specs=[pl.BlockSpec((1, D // 2, tokens), lambda i: (frames - 2 + i // 2, i % 2, 0))],
        out_specs=pl.BlockSpec((1, D // 2, tokens), lambda i: (i // 2, i % 2, 0)),
        compiler_params=limit(60),
        name="last_two",
    )(queries)


def split_kernel(row_ref, mine_ref, other_ref, own_ref, *piece_refs):
    frames = mine_ref.shape[0]
    for s in range(4):
        rows = pl.ds(pl.multiple_of(lax.rem(row_ref[0] + s, 4) * CHUNK, CHUNK), CHUNK)
        for f in range(frames):
            total = mine_ref[f, rows, :].astype(jnp.float32) + other_ref[f, rows, :].astype(jnp.float32)
            if s == 0:
                own_ref[f] = total
            elif f >= frames - 2:
                piece_refs[s - 1][f - frames + 2] = total.astype(jnp.bfloat16)
            else:
                piece_refs[s + 2][f] = total.astype(jnp.bfloat16)


def split(row, mine, other):
    frames = mine.shape[0]
    vmem = pl.BlockSpec(memory_space=pltpu.VMEM)
    return pl.pallas_call(
        split_kernel,
        out_shape=[jax.ShapeDtypeStruct((frames, CHUNK, LANES), jnp.float32)]
        + [jax.ShapeDtypeStruct((2, CHUNK, LANES), jnp.bfloat16)] * 3
        + [jax.ShapeDtypeStruct((frames - 2, CHUNK, LANES), jnp.bfloat16)] * 3,
        in_specs=[pl.BlockSpec(memory_space=pltpu.SMEM), vmem, vmem],
        out_specs=[vmem] * 7,
        compiler_params=limit(8),
        name="split",
    )(row, mine, other)


def total_kernel(own_ref, a_ref, b_ref, c_ref, sums_ref, pieces_ref):
    frames = own_ref.shape[0]
    count, rows, _ = pieces_ref.shape
    rows //= 2
    kept = []
    for f in range(2):
        total = own_ref[frames - 2 + f]
        for ref in (a_ref, b_ref, c_ref):
            total = total + ref[f].astype(jnp.float32)
        sums_ref[f] = total.astype(sums_ref.dtype)
        kept.append(total)
    earlier, last = kept
    for i in range(count):
        cut = slice(i * rows, (i + 1) * rows)
        both = jnp.concatenate([last[cut], earlier[cut]], axis=0)
        pieces_ref[i] = both.astype(pieces_ref.dtype)


def total(own, received, sections):
    vmem = pl.BlockSpec(memory_space=pltpu.VMEM)
    return pl.pallas_call(
        total_kernel,
        out_shape=[
            jax.ShapeDtypeStruct((2,) + own.shape[1:], jnp.bfloat16),
            jax.ShapeDtypeStruct((sections, 2 * CHUNK // sections, LANES), jnp.bfloat16),
        ],
        in_specs=[vmem] * 4,
        out_specs=[vmem] * 2,
        compiler_params=limit(8),
        name="total",
    )(own, *received)


def rest_kernel(own_ref, a_ref, b_ref, c_ref, last_ref, sums_ref):
    first = a_ref.shape[0]
    for f in range(first):
        total = own_ref[f]
        for ref in (a_ref, b_ref, c_ref):
            total = total + ref[f].astype(jnp.float32)
        sums_ref[f] = total.astype(sums_ref.dtype)
    for f in range(2):
        sums_ref[first + f] = last_ref[f]


def rest(own, received, last):
    vmem = pl.BlockSpec(memory_space=pltpu.VMEM)
    return pl.pallas_call(
        rest_kernel,
        out_shape=jax.ShapeDtypeStruct(own.shape, jnp.bfloat16),
        in_specs=[vmem] * 5,
        out_specs=vmem,
        compiler_params=limit(8),
        name="rest",
    )(own, *received, last)


def scan_kernel(in_ref, out_ref):
    count, rows, lanes = in_ref.shape
    rows //= 2
    before = jnp.zeros((rows, lanes), jnp.float32)
    before2 = before
    for i in range(count):
        out_ref[i] = jnp.concatenate([before, before2], axis=0).astype(out_ref.dtype)
        here = in_ref[i].astype(jnp.float32)
        before, before2 = before + here[:rows], before + here[rows:]


def exclusive_scan(value):
    vmem = pl.BlockSpec(memory_space=pltpu.VMEM)
    return pl.pallas_call(
        scan_kernel,
        out_shape=jax.ShapeDtypeStruct(value.shape, value.dtype),
        in_specs=[vmem],
        out_specs=vmem,
        compiler_params=limit(8),
        name="exclusive_scan",
    )(value)


def join_kernel(in_ref, out_ref):
    count, rows, _ = in_ref.shape
    rows //= 2
    pieces = [in_ref[i].astype(jnp.float32) for i in range(count)]
    for k in range(2):
        whole = jnp.concatenate([p[k * rows : (k + 1) * rows] for p in pieces], axis=0)
        out_ref[k] = whole.astype(out_ref.dtype)


def join(value):
    vmem = pl.BlockSpec(memory_space=pltpu.VMEM)
    return pl.pallas_call(
        join_kernel,
        out_shape=jax.ShapeDtypeStruct((2, CHUNK, LANES), value.dtype),
        in_specs=[vmem],
        out_specs=vmem,
        compiler_params=limit(8),
        name="join",
    )(value)


def pair_kernel(place_ref, mine_ref, other_ref, out_ref):
    @pl.when(place_ref[1] % 2 == 0)
    def _():
        out_ref[:PADDED] = mine_ref[...]
        out_ref[PADDED:] = other_ref[...]

    @pl.when(place_ref[1] % 2 == 1)
    def _():
        out_ref[:PADDED] = other_ref[...]
        out_ref[PADDED:] = mine_ref[...]


def in_order(place, mine, other):
    vmem = pl.BlockSpec(memory_space=pltpu.VMEM)
    return pl.pallas_call(
        pair_kernel,
        out_shape=jax.ShapeDtypeStruct((PAIR,) + mine.shape[1:], mine.dtype),
        in_specs=[pl.BlockSpec(memory_space=pltpu.SMEM), vmem, vmem],
        out_specs=vmem,
        compiler_params=limit(8),
        name="in_order",
    )(place, mine, other)


def pack_kernel(*refs):
    for i, ref in enumerate(refs[:-1]):
        refs[-1][i] = ref[...]


def pack(arrays):
    vmem = pl.BlockSpec(memory_space=pltpu.VMEM)
    return pl.pallas_call(
        pack_kernel,
        out_shape=jax.ShapeDtypeStruct((len(arrays),) + arrays[0].shape, arrays[0].dtype),
        in_specs=[vmem] * len(arrays),
        out_specs=vmem,
        compiler_params=limit(8),
        name="pack",
    )(*arrays)


def padded_row(row):
    return row + (PADDED - BLOCK) * (row // BLOCK)


def tail_kernel(spots, where_ref, *refs):
    qh_ref, q_ref = refs[:2]
    c_refs, p_refs = (refs[2:6], refs[6:10]), (refs[10:14], refs[14:18])
    count = len(spots)
    w_refs = (refs[18 : 18 + count], refs[18 + count : 18 + 2 * count])
    taps_ref, out_ref, state_ref, att_ref, weight_ref, sem = refs[18 + 2 * count :]
    step = pl.program_id(0)
    core, row = where_ref[0], where_ref[1]
    frames, width, tokens = out_ref.shape
    steps = frames + 2

    def copies():
        made = []
        for which in range(2):
            column = pl.multiple_of((which ^ core) * HALF_COLS, HALF_COLS)
            for group, places in zip(w_refs[which], spots):
                for i, (dx, dz) in enumerate(places):
                    x = lax.rem(where_ref[2] - dx + 8, 4)
                    z = lax.rem(where_ref[3] // 2 - dz + 8, 4)
                    start = pl.multiple_of((x * 4 + z) * PAIR, PAIR)
                    target = weight_ref.at[pl.ds(start, PAIR), pl.ds(column, HALF_COLS)]
                    source = group if len(places) == 1 else group.at[i]
                    made.append(pltpu.make_async_copy(source, target, sem.at[len(made)]))
        return made

    @pl.when(step == 0)
    def _():
        for copy in copies():
            copy.start()

    def fill(before, within):
        for which in range(2):
            half = which ^ core
            for s in range(4):
                chunk = lax.rem(row - s + 4, 4)
                state = p_refs[which][s][before]
                if within:
                    state = state.astype(jnp.float32) + c_refs[which][s][0].astype(jnp.float32)
                start = pl.multiple_of(chunk * CHUNK, CHUNK)
                state_ref[half, pl.ds(start, CHUNK), :] = state.astype(state_ref.dtype)

    @pl.when(step == 0)
    def _():
        fill(1, False)

    @pl.when(step == 1)
    def _():
        fill(0, False)

    @pl.when((step >= 2) & (step < steps))
    def _():
        fill(0, True)

    def heads(source):
        pad = jnp.zeros((LANES - HEAD_DIM, tokens), jnp.bfloat16)
        lanes = pl.ds(pl.multiple_of(step * tokens, tokens), tokens)
        for head in range(HEADS):
            half, inner = divmod(head, HALF_HEADS)
            query = jnp.maximum(source[0, head * HEAD_DIM : (head + 1) * HEAD_DIM, :], 0)
            first = padded_row(inner * HEAD_DIM)
            low = first // 16 * 16
            high = -(-(padded_row(inner * HEAD_DIM + HEAD_DIM - 1) + 1) // 16) * 16
            top = jnp.dot(
                state_ref[half, low:high, :],
                jnp.concatenate([query, pad], axis=0),
                preferred_element_type=jnp.float32,
            )
            norm = state_ref[half, inner * HEAD_DIM : (inner + 1) * HEAD_DIM, HEAD_DIM : HEAD_DIM + 1]
            bottom = norm.astype(jnp.float32) * query.astype(jnp.float32)
            bottom = jnp.sum(bottom, axis=0, keepdims=True) + stab_eps
            result = top * (1.0 / bottom)
            base = half * HALF_ROWS
            if first > low:
                held = att_ref[base + low : base + low + 16, lanes].astype(jnp.float32)
                keep = lax.broadcasted_iota(jnp.int32, (16, tokens), 0) < first - low
                att_ref[base + low : base + low + 16, lanes] = jnp.where(keep, held, result[:16]).astype(att_ref.dtype)
                att_ref[base + low + 16 : base + high, lanes] = result[16:].astype(att_ref.dtype)
            else:
                att_ref[base + low : base + high, lanes] = result.astype(att_ref.dtype)

    @pl.when(step < 2)
    def _():
        heads(qh_ref)

    @pl.when((step >= 2) & (step < steps))
    def _():
        heads(q_ref)

    @pl.when(step == steps)
    def _():
        for copy in copies():
            copy.wait()

    @pl.when(step >= steps)
    def _():
        column = pl.ds(pl.multiple_of((step - steps) * width, width), width)
        prod = lax.dot_general(
            weight_ref[:, column], att_ref[...], (((0,), (0,)), ((), ())), preferred_element_type=jnp.float32
        )
        prod = prod.astype(jnp.bfloat16).astype(jnp.float32)
        taps = taps_ref[...].T
        for f in range(frames):
            now, one, two = (prod[:, (f + 2 - lag) * tokens : (f + 3 - lag) * tokens] for lag in range(3))
            mixed = taps[:, 0:1] * now + taps[:, 1:2] * one + taps[:, 2:3] * two
            out_ref[f] = mixed.astype(out_ref.dtype)


def tail(where, behind, queries, c_mine, c_other, p_mine, p_other, groups, groups_other, spots, taps):
    frames, _, tokens = queries.shape
    steps = frames + 2
    own = lambda f, w: (jnp.clip(f - 2, 0, frames - 1), 0, 0)
    tile = lambda f: jnp.maximum(f - steps, 0)
    chunk = pl.BlockSpec((1, CHUNK, LANES), own)
    whole = pl.BlockSpec((2, CHUNK, LANES), lambda f, w: (0, 0, 0))
    pairs = sum(len(places) for places in spots)
    return pl.pallas_call(
        functools.partial(tail_kernel, spots),
        out_shape=jax.ShapeDtypeStruct((frames, D, tokens), jnp.bfloat16),
        grid_spec=pltpu.PrefetchScalarGridSpec(
            num_scalar_prefetch=1,
            grid=(steps + 2 * HALF_COLS // COL_TILE,),
            in_specs=[
                pl.BlockSpec((1, D, tokens), lambda f, w: (jnp.minimum(f, 1), 0, 0)),
                pl.BlockSpec((1, D, tokens), own),
            ]
            + [chunk] * 8
            + [whole] * 8
            + [pl.BlockSpec(memory_space=pl.ANY)] * (2 * len(groups))
            + [pl.BlockSpec((3, COL_TILE), lambda f, w: (0, tile(f)))],
            out_specs=pl.BlockSpec((frames, COL_TILE, tokens), lambda f, w: (0, tile(f), 0)),
            scratch_shapes=[
                pltpu.VMEM((2, HALF_ROWS, LANES), jnp.bfloat16),
                pltpu.VMEM((2 * HALF_ROWS, steps * tokens), jnp.bfloat16),
                pltpu.VMEM((2 * HALF_ROWS, 2 * HALF_COLS), jnp.bfloat16),
                pltpu.SemaphoreType.DMA((2 * pairs,)),
            ],
        ),
        compiler_params=limit(40),
        cost_estimate=pl.CostEstimate(
            flops=2 * steps * tokens * D * (D + LANES), bytes_accessed=2 * D * D, transcendentals=0
        ),
        name="tail",
    )(where, behind, queries, *c_mine, *c_other, *p_mine, *p_other, *groups, *groups_other, taps)


def layer(queries, keys, values, out_weight, conv_taps):
    nx, nz, ny = lax.axis_size("x"), lax.axis_size("z"), lax.axis_size("y")
    sections = nx * nz
    core, row = lax.axis_index("c"), lax.axis_index("y")
    place = jnp.stack([lax.axis_index("x"), lax.axis_index("z")])
    where = jnp.stack([core, row, lax.axis_index("x"), lax.axis_index("z")])
    queries, keys, values = (jnp.transpose(a, (0, 2, 1)) for a in (queries, keys, values))

    def along_y(value):
        return [shift(value, "y", s, ny) for s in range(1, ny)]

    def to_partner(arrays):
        return [shift(value, "c", 1, 2) for value in arrays]

    rows, cols = out_weight.shape
    padded = jnp.pad(out_weight, ((0, PADDED - rows), (0, 2 * HALF_COLS - cols)))
    block = lax.dynamic_slice_in_dim(padded, core * HALF_COLS, HALF_COLS, axis=1)
    partner = lax.ppermute(block, "z", [(i, i ^ 1) for i in range(nz)])
    behind = next_section(last_two(queries), sections)
    mine, theirs = local_kv(jnp.reshape(core, (1,)), keys, values)
    theirs = shift(theirs, "c", 1, 2)
    pair = in_order(place, block, after(partner, mine))
    above, below = shift(pair, "z", 2, nz), shift(pair, "z", -2, nz)
    pair_up, pair_down = shift(pair, "x", 1, nx), shift(pair, "x", -1, nx)
    own, *pieces = split(jnp.reshape(row, (1,)), mine, theirs)
    received = [shift(pieces[s - 1], "y", s, ny) for s in range(1, ny)]

    last, cuts = total(own, received, sections)
    cuts = lax.all_to_all(cuts, ("x", "z"), 0, 0)

    below = after(below, last)
    far = shift(below, "z", -2, nz)
    below_up, below_down = shift(below, "x", 1, nx), shift(below, "x", -1, nx)
    received = [shift(after(pieces[s + 2], last), "y", s, ny) for s in range(1, ny)]
    cuts = exclusive_scan(cuts)
    before = lax.all_to_all(cuts, ("x", "z"), 0, 0)
    both = pack([after(above, cuts), after(far, cuts)])
    both_up, both_down = shift(both, "x", 1, nx), shift(both, "x", -1, nx)
    sums = rest(own, [after(r, cuts) for r in received], last)
    c_mine = [sums] + along_y(sums)
    pair_two = shift(after(pair_down, cuts), "x", -1, nx)
    below_two = shift(after(below_down, cuts), "x", -1, nx)
    early = to_partner([after(a, cuts) for a in (pair, below, both, pair_up, pair_down, below_up, below_down)])

    before = join(before)
    p_mine = [before] + along_y(before)
    both_two = shift(after(both_up, before), "x", 1, nx)
    c_other = to_partner([after(a, before) for a in c_mine])
    p_other = to_partner(p_mine)
    late = to_partner([after(a, before) for a in (both_up, both_down, pair_two, below_two, both_two)])

    here, under, others = (0,), (-1,), (1, -2)
    spots = [
        [(dx, dz) for dz in steps]
        for dx, steps in (
            (0, here), (0, under), (0, others), (1, here), (-1, here), (1, under), (-1, under),
            (1, others), (-1, others), (-2, here), (-2, under), (2, others),
        )
    ]
    groups = [pair, below, both, pair_up, pair_down, below_up, below_down, both_up, both_down, pair_two, below_two, both_two]
    out = tail(where, behind, queries, c_mine, c_other, p_mine, p_other, groups, early + late, spots, conv_taps)
    return jnp.transpose(out, (0, 2, 1))


def solution(mesh):
    fine = Mesh(mesh.devices.reshape(4, 8, 4, 2), ("x", "z", "y", "c"))
    in_specs = (
        P(("x", "z"), ("y", "c"), None),
        P(("x", "z"), ("y", "c"), None),
        P(("x", "z"), ("y", "c"), None),
        P(("x", "z"), None),
        P(),
    )
    return jax.shard_map(layer, mesh=fine, in_specs=in_specs, out_specs=in_specs[0], check_vma=False)
```

profile of v0, /device:TPU:2, one launch (start us, length us, event | category | flops | bytes accessed | tf_op | source)
XLA Modules:
  0.0 170.4 jit_solution(895671409117415952)
XLA Ops:
  0.0 5.5 %local_kv.1 = (bf16[4,1152,128]{2,1,0:T(8,128)(2,1)}, bf16[4,1152,128]{2,1,0:T(8,128)(2,1)}) custom-call(s32[1]{0:T(128)} %bitcast.core_ref, bf16[4,2240,128]{2,1,0:T(8,128)(2,1)} %bitcast.8, bf16[4,2240,128]{2,1,0:T(8,128)(2,1)} %bitcast.9), custom_call_target="tpu_custom_call" | custom-call | flops 587202560 | bytes 9175040 | tf_op jit(solution)/shard_map/local_kv/pallas_call | solution.py:78
  5.5 3.5 %last_two.1 = bf16[2,2240,128]{2,1,0:T(8,128)(2,1)} custom-call(bf16[4,2240,128]{2,1,0:T(8,128)(2,1)} %bitcast.10), custom_call_target="tpu_custom_call" | custom-call | tf_op jit(solution)/shard_map/last_two/pallas_call | solution.py:102
  9.0 3.8 %collective-permute-start = (bf16[2,2240,128]{2,1,0:T(8,128)(2,1)}, bf16[2,2240,128]{2,1,0:T(8,128)(2,1)}, u32[]{:S(2)}, u32[]{:S(2)}) collective-permute-start(bf16[2,2240,128]{2,1,0:T(8,128)(2,1)} %last_two.1), channel_id=1, source_target_pairs={{0,8},{8,16},{16,24},{24,32},{32,40},{40,48},{48,56},{56,64},{64,7... | collective-permute-start | bytes 3440648 | tf_op jit(solution)/shard_map/ppermute | solution.py:31
  12.9 2.0 %collective-permute-start.22 = (bf16[72,1152]{1,0:T(8,128)(2,1)S(1)}, bf16[72,1152]{1,0:T(8,128)(2,1)S(1)}, u32[]{:S(2)}, u32[]{:S(2)}) collective-permute-start(bf16[72,1152]{1,0:T(8,128)(2,1)S(1)} %pad_dynamic-slice_fusion.mine_ref), channel_id=1, source_target_pairs={{0,8},{8,0},{16,24},{24,16},{32,40},{40,32},{48,56},{56,48},{1,9},... | collective-permute-start | bytes 497672 | tf_op jit(solution)/shard_map/ppermute | solution.py:449
  14.9 0.8 split.1
  15.8 0.7 copy-done.1
  16.4 0.7 copy-done.3
  17.1 1.6 collective-permute-start.2
  18.7 2.9 %collective-permute-start.3 = (bf16[2,288,128]{2,1,0:T(8,128)(2,1)S(1)}, bf16[2,288,128]{2,1,0:T(8,128)(2,1)S(1)}, u32[]{:S(2)}, u32[]{:S(2)}) collective-permute-start(bf16[2,288,128]{2,1,0:T(8,128)(2,1)S(1)} %get-tuple-element.47), channel_id=1, source_target_pairs={{0,4},{2,6},{4,0},{6,2},{1,5},{3,7},{5,1},{7,3},{8,12},{10,14},{12... | collective-permute-start | bytes 442376 | tf_op jit(solution)/shard_map/ppermute | solution.py:27
  21.6 20.1 %collective-permute-done.22.other_ref = bf16[72,1152]{1,0:T(8,128)(2,1)S(1)} collective-permute-done((bf16[72,1152]{1,0:T(8,128)(2,1)S(1)}, bf16[72,1152]{1,0:T(8,128)(2,1)S(1)}, u32[]{:S(2)}, u32[]{:S(2)}) %collective-permute-start.22) | collective-permute-done | bytes 165920 | tf_op jit(solution)/shard_map/ppermute | solution.py:449
  41.8 0.6 in_order.1.refs_18_
  42.3 5.5 %collective-permute-start.23 = (bf16[144,1152]{1,0:T(8,128)(2,1)S(1)}, bf16[144,1152]{1,0:T(8,128)(2,1)S(1)}, u32[]{:S(2)}, u32[]{:S(2)}) collective-permute-start(bf16[144,1152]{1,0:T(8,128)(2,1)S(1)} %in_order.1.refs_18_), channel_id=1, source_target_pairs={{0,48},{8,56},{16,0},{24,8},{32,16},{40,24},{48,32},{56,40},{1,49}... | collective-permute-start | bytes 995336 | tf_op jit(solution)/shard_map/ppermute | solution.py:27
  47.8 0.5 collective-permute-start.27
  48.4 3.1 %collective-permute-start.4 = (bf16[2,288,128]{2,1,0:T(8,128)(2,1)S(1)}, bf16[2,288,128]{2,1,0:T(8,128)(2,1)S(1)}, u32[]{:S(2)}, u32[]{:S(2)}) collective-permute-start(bf16[2,288,128]{2,1,0:T(8,128)(2,1)S(1)} %get-tuple-element.48), channel_id=1, source_target_pairs={{0,6},{2,0},{4,2},{6,4},{1,7},{3,1},{5,3},{7,5},{8,14},{10,8},{12,... | collective-permute-start | bytes 442376 | tf_op jit(solution)/shard_map/ppermute | solution.py:27
  51.5 2.7 %collective-permute-done.4.c_ref = bf16[2,288,128]{2,1,0:T(8,128)(2,1)S(1)} collective-permute-done((bf16[2,288,128]{2,1,0:T(8,128)(2,1)S(1)}, bf16[2,288,128]{2,1,0:T(8,128)(2,1)S(1)}, u32[]{:S(2)}, u32[]{:S(2)}) %collective-permute-start.4) | collective-permute-done | bytes 147488 | tf_op jit(solution)/shard_map/ppermute | solution.py:27
  54.1 0.8 total.1
  54.9 1.0 collective-permute-start.5
  56.0 6.7 %collective-permute-done.23.refs_19_ = bf16[144,1152]{1,0:T(8,128)(2,1)S(1)} collective-permute-done((bf16[144,1152]{1,0:T(8,128)(2,1)S(1)}, bf16[144,1152]{1,0:T(8,128)(2,1)S(1)}, u32[]{:S(2)}, u32[]{:S(2)}) %collective-permute-start.23) | collective-permute-done | bytes 331808 | tf_op jit(solution)/shard_map/ppermute | solution.py:27
  62.7 4.6 %collective-permute-start.25 = (bf16[144,1152]{1,0:T(8,128)(2,1)S(1)}, bf16[144,1152]{1,0:T(8,128)(2,1)S(1)}, u32[]{:S(2)}, u32[]{:S(2)}) collective-permute-start(bf16[144,1152]{1,0:T(8,128)(2,1)S(1)} %collective-permute-done.23.refs_19_), channel_id=1, source_target_pairs={{0,48},{8,56},{16,0},{24,8},{32,16},{40,24},{48,32},{56,40},{1,49}... | collective-permute-start | bytes 995336 | tf_op jit(solution)/shard_map/ppermute | solution.py:27
  67.3 6.0 %all-to-all-start = ((bf16[32,18,128]{2,1,0:T(8,128)(2,1)}), bf16[32,18,128]{2,1,0:T(8,128)(2,1)S(1)}, u32[]{:S(2)}, u32[]{:S(2)}) async-start(bf16[32,18,128]{2,1,0:T(8,128)(2,1)} %get-tuple-element.51), calls=%async_computation | async-start | bytes 393216 | tf_op jit(solution)/shard_map/all_to_all | solution.py:460
  73.3 3.3 %collective-permute-start.6 = (bf16[2,288,128]{2,1,0:T(8,128)(2,1)S(1)}, bf16[2,288,128]{2,1,0:T(8,128)(2,1)S(1)}, u32[]{:S(2)}, u32[]{:S(2)}) collective-permute-start(bf16[2,288,128]{2,1,0:T(8,128)(2,1)S(1)} %copy-done.4), channel_id=1, source_target_pairs={{0,4},{2,6},{4,0},{6,2},{1,5},{3,7},{5,1},{7,3},{8,12},{10,14},{12... | collective-permute-start | bytes 442376 | tf_op jit(solution)/shard_map/ppermute | solution.py:27
  76.6 1.1 collective-permute-start.7
  77.6 1.5 collective-permute-start.26
  79.1 0.9 collective-permute-done.6.b_ref
  80.0 0.3 collective-permute-start.29
  80.3 3.0 %collective-permute-done.7.c_ref = bf16[2,288,128]{2,1,0:T(8,128)(2,1)S(1)} collective-permute-done((bf16[2,288,128]{2,1,0:T(8,128)(2,1)S(1)}, bf16[2,288,128]{2,1,0:T(8,128)(2,1)S(1)}, u32[]{:S(2)}, u32[]{:S(2)}) %collective-permute-start.7) | collective-permute-done | bytes 147488 | tf_op jit(solution)/shard_map/ppermute | solution.py:27
  83.3 1.5 collective-permute-start.28
  84.8 0.2 all-to-all-done.in_ref
  85.0 0.7 exclusive_scan.1
  85.8 3.1 %collective-permute-start.10 = (bf16[4,288,128]{2,1,0:T(8,128)(2,1)S(1)}, bf16[4,288,128]{2,1,0:T(8,128)(2,1)}, u32[]{:S(2)}, u32[]{:S(2)}) collective-permute-start(bf16[4,288,128]{2,1,0:T(8,128)(2,1)S(1)} %rest.1.refs_2_), channel_id=1, source_target_pairs={{0,6},{2,0},{4,2},{6,4},{1,7},{3,1},{5,3},{7,5},{8,14},{10,8},{12,... | collective-permute-start | bytes 884744 | tf_op jit(solution)/shard_map/ppermute | solution.py:27
  89.0 1.3 collective-permute-start.30
  90.3 1.9 %collective-permute-start.9 = (bf16[4,288,128]{2,1,0:T(8,128)(2,1)S(1)}, bf16[4,288,128]{2,1,0:T(8,128)(2,1)S(1)}, u32[]{:S(2)}, u32[]{:S(2)}) collective-permute-start(bf16[4,288,128]{2,1,0:T(8,128)(2,1)S(1)} %rest.1.refs_2_), channel_id=1, source_target_pairs={{0,4},{2,6},{4,0},{6,2},{1,5},{3,7},{5,1},{7,3},{8,12},{10,14},{12... | collective-permute-start | bytes 884744 | tf_op jit(solution)/shard_map/ppermute | solution.py:27
  92.3 3.7 %collective-permute-done.28.refs_23_ = bf16[144,1152]{1,0:T(8,128)(2,1)} collective-permute-done((bf16[144,1152]{1,0:T(8,128)(2,1)S(1)}, bf16[144,1152]{1,0:T(8,128)(2,1)}, u32[]{:S(2)}, u32[]{:S(2)}) %collective-permute-start.28) | collective-permute-done | bytes 331808 | tf_op jit(solution)/shard_map/ppermute | solution.py:27
  96.0 0.9 collective-permute-start.8
  96.9 4.4 %collective-permute-done.10.refs_5_ = bf16[4,288,128]{2,1,0:T(8,128)(2,1)} collective-permute-done((bf16[4,288,128]{2,1,0:T(8,128)(2,1)S(1)}, bf16[4,288,128]{2,1,0:T(8,128)(2,1)}, u32[]{:S(2)}, u32[]{:S(2)}) %collective-permute-start.10) | collective-permute-done | bytes 294944 | tf_op jit(solution)/shard_map/ppermute | solution.py:27
  101.3 1.4 collective-permute-start.32
  102.7 3.0 %collective-permute-done.8.refs_3_ = bf16[4,288,128]{2,1,0:T(8,128)(2,1)} collective-permute-done((bf16[4,288,128]{2,1,0:T(8,128)(2,1)S(1)}, bf16[4,288,128]{2,1,0:T(8,128)(2,1)}, u32[]{:S(2)}, u32[]{:S(2)}) %collective-permute-start.8) | collective-permute-done | bytes 294944 | tf_op jit(solution)/shard_map/ppermute | solution.py:27
  105.7 0.5 collective-permute-start.38
  106.3 8.9 %all-to-all-start.1 = ((bf16[32,18,128]{2,1,0:T(8,128)(2,1)}), bf16[32,18,128]{2,1,0:T(8,128)(2,1)S(1)}, u32[]{:S(2)}, u32[]{:S(2)}) async-start(bf16[32,18,128]{2,1,0:T(8,128)(2,1)} %exclusive_scan.1), calls=%async_computation.1 | async-start | bytes 393216 | tf_op jit(solution)/shard_map/all_to_all | solution.py:467
  115.3 0.3 collective-permute-start.33
  115.6 0.3 collective-permute-start.40
  115.8 9.7 %all-to-all-done.1.in_ref = bf16[32,18,128]{2,1,0:T(8,128)(2,1)S(1)} async-done(((bf16[32,18,128]{2,1,0:T(8,128)(2,1)}), bf16[32,18,128]{2,1,0:T(8,128)(2,1)S(1)}, u32[]{:S(2)}, u32[]{:S(2)}) %all-to-all-start.1) | async-done | bytes 147488 | tf_op jit(solution)/shard_map/all_to_all | solution.py:467
  125.6 1.4 collective-permute-start.31
  127.0 0.7 collective-permute-start.34
  127.7 0.4 collective-permute-done.33.refs_28_
  128.1 0.3 collective-permute-start.17
  128.4 0.7 collective-permute-done.18.refs_14_
  129.1 1.5 collective-permute-start.16
  130.6 4.2 %collective-permute-done.17.refs_13_ = bf16[2,288,128]{2,1,0:T(8,128)(2,1)S(1)} collective-permute-done((bf16[2,288,128]{2,1,0:T(8,128)(2,1)S(1)}, bf16[2,288,128]{2,1,0:T(8,128)(2,1)S(1)}, u32[]{:S(2)}, u32[]{:S(2)}) %collective-permute-start.17) | collective-permute-done | bytes 147488 | tf_op jit(solution)/shard_map/ppermute | solution.py:27
  134.8 1.7 collective-permute-done.16.refs_12_
  136.5 4.7 %collective-permute-done.15.refs_11_ = bf16[2,288,128]{2,1,0:T(8,128)(2,1)S(1)} collective-permute-done((bf16[2,288,128]{2,1,0:T(8,128)(2,1)S(1)}, bf16[2,288,128]{2,1,0:T(8,128)(2,1)S(1)}, u32[]{:S(2)}, u32[]{:S(2)}) %collective-permute-start.15) | collective-permute-done | bytes 147488 | tf_op jit(solution)/shard_map/ppermute | solution.py:27
  141.2 0.5 collective-permute-start.13
  141.8 0.4 collective-permute-start.20
  142.2 0.1 collective-permute-start.19
  142.3 1.7 collective-permute-done.20.refs_16_
  144.0 0.1 collective-permute-start.37
  144.2 0.3 collective-permute-start.44
  144.5 0.2 collective-permute-start.42
  144.7 0.3 collective-permute-start.43
  145.0 0.2 collective-permute-start.46
  145.2 1.3 collective-permute-done.44.refs_39_
  146.6 0.1 collective-permute-start.45
  146.8 3.1 %collective-permute-done.45.refs_40_ = bf16[144,1152]{1,0:T(8,128)(2,1)S(1)} collective-permute-done((bf16[144,1152]{1,0:T(8,128)(2,1)}, bf16[144,1152]{1,0:T(8,128)(2,1)S(1)}, u32[]{:S(2)}, u32[]{:S(2)}) %collective-permute-start.45) | collective-permute-done | bytes 331808 | tf_op jit(solution)/shard_map/ppermute | solution.py:27
  149.9 20.3 %tail.1 = bf16[4,2240,128]{2,1,0:T(8,128)(2,1)} custom-call(s32[4]{0:T(128)S(1)} %pad_add_fusion.where_ref, bf16[2,2240,128]{2,1,0:T(8,128)(2,1)} %collective-permute-done.refs_0_, bf16[4,2240,128]{2,1,0:T(8,128)(2,1)} %bitcast.11, bf16[4,288,128]{2,1,0:T(8,128)(2,1)S(1)} %rest.1.refs_2_, bf16[4,288,128]{2,1,0:T(8,128)(2,1)} %collective-permute-done.8.refs_3_, ...), custom_call_target="tpu_custom_call" | custom-call | flops 8147435520 | bytes 10035200 | tf_op jit(solution)/shard_map/tail/pallas_call | solution.py:402
  (61 shorter events, 0.8 us)
Async XLA Ops:
  5.5 9.4 %collective-permute-start.1 = (bf16[4,1152,128]{2,1,0:T(8,128)(2,1)}, bf16[4,1152,128]{2,1,0:T(8,128)(2,1)S(1)}, u32[]{:S(2)}, u32[]{:S(2)}) collective-permute-start(bf16[4,1152,128]{2,1,0:T(8,128)(2,1)} %get-tuple-element.43), channel_id=1, source_target_pairs={{0,1},{1,0},{2,3},{3,2},{4,5},{5,4},{6,7},{7,6},{8,9},{9,8},{10,11... | collective-permute-start | bytes 3538952 | tf_op jit(solution)/shard_map/ppermute | solution.py:27
  5.5 7.4 %copy-start.6 = (bf16[70,2240]{1,0:T(8,128)(2,1)S(1)}, bf16[70,2240]{1,0:T(8,128)(2,1)}, u32[]{:S(2)}) copy-start(bf16[70,2240]{1,0:T(8,128)(2,1)} %param.8) | copy-start | bytes 940804
  5.5 9.4 %copy-start = (bf16[4,1152,128]{2,1,0:T(8,128)(2,1)S(1)}, bf16[4,1152,128]{2,1,0:T(8,128)(2,1)}, u32[]{:S(2)}) copy-start(bf16[4,1152,128]{2,1,0:T(8,128)(2,1)} %get-tuple-element.42.mine_ref) | copy-start | bytes 3538948
  9.0 81.3 %collective-permute-start = (bf16[2,2240,128]{2,1,0:T(8,128)(2,1)}, bf16[2,2240,128]{2,1,0:T(8,128)(2,1)}, u32[]{:S(2)}, u32[]{:S(2)}) collective-permute-start(bf16[2,2240,128]{2,1,0:T(8,128)(2,1)} %last_two.1), channel_id=1, source_target_pairs={{0,8},{8,16},{16,24},{24,32},{32,40},{40,48},{48,56},{56,64},{64,7... | collective-permute-start | bytes 3440648 | tf_op jit(solution)/shard_map/ppermute | solution.py:31
  12.9 28.8 %collective-permute-start.22 = (bf16[72,1152]{1,0:T(8,128)(2,1)S(1)}, bf16[72,1152]{1,0:T(8,128)(2,1)S(1)}, u32[]{:S(2)}, u32[]{:S(2)}) collective-permute-start(bf16[72,1152]{1,0:T(8,128)(2,1)S(1)} %pad_dynamic-slice_fusion.mine_ref), channel_id=1, source_target_pairs={{0,8},{8,0},{16,24},{24,16},{32,40},{40,32},{48,56},{56,48},{1,9},... | collective-permute-start | bytes 497672 | tf_op jit(solution)/shard_map/ppermute | solution.py:449
  15.8 0.7 copy-start.1
  16.4 0.7 copy-start.3
  17.1 56.2 %copy-start.4 = (bf16[2,288,128]{2,1,0:T(8,128)(2,1)S(1)}, bf16[2,288,128]{2,1,0:T(8,128)(2,1)}, u32[]{:S(2)}) copy-start(bf16[2,288,128]{2,1,0:T(8,128)(2,1)} %copy-done.3) | copy-start | bytes 442372
  17.1 59.5 %copy-start.2 = (bf16[2,288,128]{2,1,0:T(8,128)(2,1)S(1)}, bf16[2,288,128]{2,1,0:T(8,128)(2,1)}, u32[]{:S(2)}) copy-start(bf16[2,288,128]{2,1,0:T(8,128)(2,1)} %copy-done.1) | copy-start | bytes 442372
  17.1 31.3 %collective-permute-start.2 = (bf16[2,288,128]{2,1,0:T(8,128)(2,1)S(1)}, bf16[2,288,128]{2,1,0:T(8,128)(2,1)S(1)}, u32[]{:S(2)}, u32[]{:S(2)}) collective-permute-start(bf16[2,288,128]{2,1,0:T(8,128)(2,1)S(1)} %get-tuple-element.46), channel_id=1, source_target_pairs={{0,2},{2,4},{4,6},{6,0},{1,3},{3,5},{5,7},{7,1},{8,10},{10,12},{12... | collective-permute-start | bytes 442376 | tf_op jit(solution)/shard_map/ppermute | solution.py:27
  18.7 29.7 %collective-permute-start.3 = (bf16[2,288,128]{2,1,0:T(8,128)(2,1)S(1)}, bf16[2,288,128]{2,1,0:T(8,128)(2,1)S(1)}, u32[]{:S(2)}, u32[]{:S(2)}) collective-permute-start(bf16[2,288,128]{2,1,0:T(8,128)(2,1)S(1)} %get-tuple-element.47), channel_id=1, source_target_pairs={{0,4},{2,6},{4,0},{6,2},{1,5},{3,7},{5,1},{7,3},{8,12},{10,14},{12... | collective-permute-start | bytes 442376 | tf_op jit(solution)/shard_map/ppermute | solution.py:27
  42.3 20.3 %collective-permute-start.23 = (bf16[144,1152]{1,0:T(8,128)(2,1)S(1)}, bf16[144,1152]{1,0:T(8,128)(2,1)S(1)}, u32[]{:S(2)}, u32[]{:S(2)}) collective-permute-start(bf16[144,1152]{1,0:T(8,128)(2,1)S(1)} %in_order.1.refs_18_), channel_id=1, source_target_pairs={{0,48},{8,56},{16,0},{24,8},{32,16},{40,24},{48,32},{56,40},{1,49}... | collective-permute-start | bytes 995336 | tf_op jit(solution)/shard_map/ppermute | solution.py:27
  47.8 25.4 %collective-permute-start.27 = (bf16[144,1152]{1,0:T(8,128)(2,1)S(1)}, bf16[144,1152]{1,0:T(8,128)(2,1)S(1)}, u32[]{:S(2)}, u32[]{:S(2)}) collective-permute-start(bf16[144,1152]{1,0:T(8,128)(2,1)S(1)} %in_order.1.refs_18_), channel_id=1, source_target_pairs={{0,192},{64,0},{128,64},{192,128},{1,193},{65,1},{129,65},{193,129... | collective-permute-start | bytes 995336 | tf_op jit(solution)/shard_map/ppermute | solution.py:27
  48.4 28.2 %collective-permute-start.24 = (bf16[144,1152]{1,0:T(8,128)(2,1)S(1)}, bf16[144,1152]{1,0:T(8,128)(2,1)S(1)}, u32[]{:S(2)}, u32[]{:S(2)}) collective-permute-start(bf16[144,1152]{1,0:T(8,128)(2,1)S(1)} %in_order.1.refs_18_), channel_id=1, source_target_pairs={{0,16},{8,24},{16,32},{24,40},{32,48},{40,56},{48,0},{56,8},{1,17}... | collective-permute-start | bytes 995336 | tf_op jit(solution)/shard_map/ppermute | solution.py:27
  48.4 5.8 %collective-permute-start.4 = (bf16[2,288,128]{2,1,0:T(8,128)(2,1)S(1)}, bf16[2,288,128]{2,1,0:T(8,128)(2,1)S(1)}, u32[]{:S(2)}, u32[]{:S(2)}) collective-permute-start(bf16[2,288,128]{2,1,0:T(8,128)(2,1)S(1)} %get-tuple-element.48), channel_id=1, source_target_pairs={{0,6},{2,0},{4,2},{6,4},{1,7},{3,1},{5,3},{7,5},{8,14},{10,8},{12,... | collective-permute-start | bytes 442376 | tf_op jit(solution)/shard_map/ppermute | solution.py:27
  54.9 22.7 %collective-permute-start.5 = (bf16[2,288,128]{2,1,0:T(8,128)(2,1)}, bf16[2,288,128]{2,1,0:T(8,128)(2,1)S(1)}, u32[]{:S(2)}, u32[]{:S(2)}) collective-permute-start(bf16[2,288,128]{2,1,0:T(8,128)(2,1)} %get-tuple-element.50), channel_id=1, source_target_pairs={{0,2},{2,4},{4,6},{6,0},{1,3},{3,5},{5,7},{7,1},{8,10},{10,12},{12... | collective-permute-start | bytes 442376 | tf_op jit(solution)/shard_map/ppermute | solution.py:27
  62.7 23.2 %collective-permute-start.25 = (bf16[144,1152]{1,0:T(8,128)(2,1)S(1)}, bf16[144,1152]{1,0:T(8,128)(2,1)S(1)}, u32[]{:S(2)}, u32[]{:S(2)}) collective-permute-start(bf16[144,1152]{1,0:T(8,128)(2,1)S(1)} %collective-permute-done.23.refs_19_), channel_id=1, source_target_pairs={{0,48},{8,56},{16,0},{24,8},{32,16},{40,24},{48,32},{56,40},{1,49}... | collective-permute-start | bytes 995336 | tf_op jit(solution)/shard_map/ppermute | solution.py:27
  67.3 17.7 %all-to-all-start = ((bf16[32,18,128]{2,1,0:T(8,128)(2,1)}), bf16[32,18,128]{2,1,0:T(8,128)(2,1)S(1)}, u32[]{:S(2)}, u32[]{:S(2)}) async-start(bf16[32,18,128]{2,1,0:T(8,128)(2,1)} %get-tuple-element.51), calls=%async_computation | async-start | bytes 393216 | tf_op jit(solution)/shard_map/all_to_all | solution.py:460
  73.3 6.7 %collective-permute-start.6 = (bf16[2,288,128]{2,1,0:T(8,128)(2,1)S(1)}, bf16[2,288,128]{2,1,0:T(8,128)(2,1)S(1)}, u32[]{:S(2)}, u32[]{:S(2)}) collective-permute-start(bf16[2,288,128]{2,1,0:T(8,128)(2,1)S(1)} %copy-done.4), channel_id=1, source_target_pairs={{0,4},{2,6},{4,0},{6,2},{1,5},{3,7},{5,1},{7,3},{8,12},{10,14},{12... | collective-permute-start | bytes 442376 | tf_op jit(solution)/shard_map/ppermute | solution.py:27
  76.6 6.7 %collective-permute-start.7 = (bf16[2,288,128]{2,1,0:T(8,128)(2,1)S(1)}, bf16[2,288,128]{2,1,0:T(8,128)(2,1)S(1)}, u32[]{:S(2)}, u32[]{:S(2)}) collective-permute-start(bf16[2,288,128]{2,1,0:T(8,128)(2,1)S(1)} %copy-done.2), channel_id=1, source_target_pairs={{0,6},{2,0},{4,2},{6,4},{1,7},{3,1},{5,3},{7,5},{8,14},{10,8},{12,... | collective-permute-start | bytes 442376 | tf_op jit(solution)/shard_map/ppermute | solution.py:27
  77.6 11.4 %collective-permute-start.26 = (bf16[144,1152]{1,0:T(8,128)(2,1)S(1)}, bf16[144,1152]{1,0:T(8,128)(2,1)}, u32[]{:S(2)}, u32[]{:S(2)}) collective-permute-start(bf16[144,1152]{1,0:T(8,128)(2,1)S(1)} %in_order.1.refs_18_), channel_id=1, source_target_pairs={{0,64},{64,128},{128,192},{192,0},{1,65},{65,129},{129,193},{193,1... | collective-permute-start | bytes 995336 | tf_op jit(solution)/shard_map/ppermute | solution.py:27
  80.0 12.3 %collective-permute-start.29 = (bf16[144,1152]{1,0:T(8,128)(2,1)S(1)}, bf16[144,1152]{1,0:T(8,128)(2,1)}, u32[]{:S(2)}, u32[]{:S(2)}) collective-permute-start(bf16[144,1152]{1,0:T(8,128)(2,1)S(1)} %collective-permute-done.23.refs_19_), channel_id=1, source_target_pairs={{0,192},{64,0},{128,64},{192,128},{1,193},{65,1},{129,65},{193,129... | collective-permute-start | bytes 995336 | tf_op jit(solution)/shard_map/ppermute | solution.py:27
  83.3 12.7 %collective-permute-start.28 = (bf16[144,1152]{1,0:T(8,128)(2,1)S(1)}, bf16[144,1152]{1,0:T(8,128)(2,1)}, u32[]{:S(2)}, u32[]{:S(2)}) collective-permute-start(bf16[144,1152]{1,0:T(8,128)(2,1)S(1)} %collective-permute-done.23.refs_19_), channel_id=1, source_target_pairs={{0,64},{64,128},{128,192},{192,0},{1,65},{65,129},{129,193},{193,1... | collective-permute-start | bytes 995336 | tf_op jit(solution)/shard_map/ppermute | solution.py:27
  85.8 64.1 %copy-start.5 = (f32[3,2240]{1,0:T(4,128)S(1)}, f32[3,2240]{1,0:T(4,128)}, u32[]{:S(2)}) copy-start(f32[3,2240]{1,0:T(4,128)} %refs_42_.1) | copy-start | bytes 80644
  85.8 15.4 %collective-permute-start.10 = (bf16[4,288,128]{2,1,0:T(8,128)(2,1)S(1)}, bf16[4,288,128]{2,1,0:T(8,128)(2,1)}, u32[]{:S(2)}, u32[]{:S(2)}) collective-permute-start(bf16[4,288,128]{2,1,0:T(8,128)(2,1)S(1)} %rest.1.refs_2_), channel_id=1, source_target_pairs={{0,6},{2,0},{4,2},{6,4},{1,7},{3,1},{5,3},{7,5},{8,14},{10,8},{12,... | collective-permute-start | bytes 884744 | tf_op jit(solution)/shard_map/ppermute | solution.py:27
  89.0 26.6 %collective-permute-start.30 = (bf16[2,144,1152]{2,1,0:T(8,128)(2,1)S(1)}, bf16[2,144,1152]{2,1,0:T(8,128)(2,1)S(1)}, u32[]{:S(2)}, u32[]{:S(2)}) collective-permute-start(bf16[2,144,1152]{2,1,0:T(8,128)(2,1)S(1)} %pack.1.refs_20_), channel_id=1, source_target_pairs={{0,64},{64,128},{128,192},{192,0},{1,65},{65,129},{129,193},{193,1... | collective-permute-start | bytes 1990664 | tf_op jit(solution)/shard_map/ppermute | solution.py:27
  90.3 12.4 %collective-permute-start.9 = (bf16[4,288,128]{2,1,0:T(8,128)(2,1)S(1)}, bf16[4,288,128]{2,1,0:T(8,128)(2,1)S(1)}, u32[]{:S(2)}, u32[]{:S(2)}) collective-permute-start(bf16[4,288,128]{2,1,0:T(8,128)(2,1)S(1)} %rest.1.refs_2_), channel_id=1, source_target_pairs={{0,4},{2,6},{4,0},{6,2},{1,5},{3,7},{5,1},{7,3},{8,12},{10,14},{12... | collective-permute-start | bytes 884744 | tf_op jit(solution)/shard_map/ppermute | solution.py:27
  92.3 13.5 %collective-permute-start.39 = (bf16[144,1152]{1,0:T(8,128)(2,1)S(1)}, bf16[144,1152]{1,0:T(8,128)(2,1)S(1)}, u32[]{:S(2)}, u32[]{:S(2)}) collective-permute-start(bf16[144,1152]{1,0:T(8,128)(2,1)S(1)} %collective-permute-done.27.refs_22_), channel_id=1, source_target_pairs={{0,1},{1,0},{2,3},{3,2},{4,5},{5,4},{6,7},{7,6},{8,9},{9,8},{10,11... | collective-permute-start | bytes 995336 | tf_op jit(solution)/shard_map/ppermute | solution.py:27
  96.0 9.8 %collective-permute-start.8 = (bf16[4,288,128]{2,1,0:T(8,128)(2,1)S(1)}, bf16[4,288,128]{2,1,0:T(8,128)(2,1)}, u32[]{:S(2)}, u32[]{:S(2)}) collective-permute-start(bf16[4,288,128]{2,1,0:T(8,128)(2,1)S(1)} %rest.1.refs_2_), channel_id=1, source_target_pairs={{0,2},{2,4},{4,6},{6,0},{1,3},{3,5},{5,7},{7,1},{8,10},{10,12},{12... | collective-permute-start | bytes 884744 | tf_op jit(solution)/shard_map/ppermute | solution.py:27
  101.3 13.9 %collective-permute-start.32 = (bf16[144,1152]{1,0:T(8,128)(2,1)S(1)}, bf16[144,1152]{1,0:T(8,128)(2,1)}, u32[]{:S(2)}, u32[]{:S(2)}) collective-permute-start(bf16[144,1152]{1,0:T(8,128)(2,1)S(1)} %collective-permute-done.27.refs_22_), channel_id=1, source_target_pairs={{0,192},{64,0},{128,64},{192,128},{1,193},{65,1},{129,65},{193,129... | collective-permute-start | bytes 995336 | tf_op jit(solution)/shard_map/ppermute | solution.py:27
  102.7 12.5 %collective-permute-start.35 = (bf16[144,1152]{1,0:T(8,128)(2,1)S(1)}, bf16[144,1152]{1,0:T(8,128)(2,1)}, u32[]{:S(2)}, u32[]{:S(2)}) collective-permute-start(bf16[144,1152]{1,0:T(8,128)(2,1)S(1)} %in_order.1.refs_18_), channel_id=1, source_target_pairs={{0,1},{1,0},{2,3},{3,2},{4,5},{5,4},{6,7},{7,6},{8,9},{9,8},{10,11... | collective-permute-start | bytes 995336 | tf_op jit(solution)/shard_map/ppermute | solution.py:27
  105.7 19.8 %collective-permute-start.36 = (bf16[144,1152]{1,0:T(8,128)(2,1)S(1)}, bf16[144,1152]{1,0:T(8,128)(2,1)}, u32[]{:S(2)}, u32[]{:S(2)}) collective-permute-start(bf16[144,1152]{1,0:T(8,128)(2,1)S(1)} %collective-permute-done.23.refs_19_), channel_id=1, source_target_pairs={{0,1},{1,0},{2,3},{3,2},{4,5},{5,4},{6,7},{7,6},{8,9},{9,8},{10,11... | collective-permute-start | bytes 995336 | tf_op jit(solution)/shard_map/ppermute | solution.py:27
  105.7 21.2 %collective-permute-start.38 = (bf16[144,1152]{1,0:T(8,128)(2,1)}, bf16[144,1152]{1,0:T(8,128)(2,1)}, u32[]{:S(2)}, u32[]{:S(2)}) collective-permute-start(bf16[144,1152]{1,0:T(8,128)(2,1)} %collective-permute-done.26.refs_21_), channel_id=1, source_target_pairs={{0,1},{1,0},{2,3},{3,2},{4,5},{5,4},{6,7},{7,6},{8,9},{9,8},{10,11... | collective-permute-start | bytes 995336 | tf_op jit(solution)/shard_map/ppermute | solution.py:27
  106.3 19.3 %all-to-all-start.1 = ((bf16[32,18,128]{2,1,0:T(8,128)(2,1)}), bf16[32,18,128]{2,1,0:T(8,128)(2,1)S(1)}, u32[]{:S(2)}, u32[]{:S(2)}) async-start(bf16[32,18,128]{2,1,0:T(8,128)(2,1)} %exclusive_scan.1), calls=%async_computation.1 | async-start | bytes 393216 | tf_op jit(solution)/shard_map/all_to_all | solution.py:467
  115.1 12.6 %collective-permute-start.41 = (bf16[144,1152]{1,0:T(8,128)(2,1)}, bf16[144,1152]{1,0:T(8,128)(2,1)}, u32[]{:S(2)}, u32[]{:S(2)}) collective-permute-start(bf16[144,1152]{1,0:T(8,128)(2,1)} %collective-permute-done.29.refs_24_), channel_id=1, source_target_pairs={{0,1},{1,0},{2,3},{3,2},{4,5},{5,4},{6,7},{7,6},{8,9},{9,8},{10,11... | collective-permute-start | bytes 995336 | tf_op jit(solution)/shard_map/ppermute | solution.py:27
  115.3 12.8 %collective-permute-start.33 = (bf16[144,1152]{1,0:T(8,128)(2,1)}, bf16[144,1152]{1,0:T(8,128)(2,1)}, u32[]{:S(2)}, u32[]{:S(2)}) collective-permute-start(bf16[144,1152]{1,0:T(8,128)(2,1)} %collective-permute-done.29.refs_24_), channel_id=1, source_target_pairs={{0,192},{64,0},{128,64},{192,128},{1,193},{65,1},{129,65},{193,129... | collective-permute-start | bytes 995336 | tf_op jit(solution)/shard_map/ppermute | solution.py:27
  115.6 12.8 %collective-permute-start.40 = (bf16[144,1152]{1,0:T(8,128)(2,1)}, bf16[144,1152]{1,0:T(8,128)(2,1)}, u32[]{:S(2)}, u32[]{:S(2)}) collective-permute-start(bf16[144,1152]{1,0:T(8,128)(2,1)} %collective-permute-done.28.refs_23_), channel_id=1, source_target_pairs={{0,1},{1,0},{2,3},{3,2},{4,5},{5,4},{6,7},{7,6},{8,9},{9,8},{10,11... | collective-permute-start | bytes 995336 | tf_op jit(solution)/shard_map/ppermute | solution.py:27
  125.6 16.2 %collective-permute-start.31 = (bf16[2,144,1152]{2,1,0:T(8,128)(2,1)S(1)}, bf16[2,144,1152]{2,1,0:T(8,128)(2,1)S(1)}, u32[]{:S(2)}, u32[]{:S(2)}) collective-permute-start(bf16[2,144,1152]{2,1,0:T(8,128)(2,1)S(1)} %pack.1.refs_20_), channel_id=1, source_target_pairs={{0,192},{64,0},{128,64},{192,128},{1,193},{65,1},{129,65},{193,129... | collective-permute-start | bytes 1990664 | tf_op jit(solution)/shard_map/ppermute | solution.py:27
  127.0 15.2 %collective-permute-start.34 = (bf16[2,144,1152]{2,1,0:T(8,128)(2,1)S(1)}, bf16[2,144,1152]{2,1,0:T(8,128)(2,1)S(1)}, u32[]{:S(2)}, u32[]{:S(2)}) collective-permute-start(bf16[2,144,1152]{2,1,0:T(8,128)(2,1)S(1)} %collective-permute-done.30.refs_25_), channel_id=1, source_target_pairs={{0,64},{64,128},{128,192},{192,0},{1,65},{65,129},{129,193},{193,1... | collective-permute-start | bytes 1990664 | tf_op jit(solution)/shard_map/ppermute | solution.py:27
  127.7 1.4 collective-permute-start.18
  128.1 6.7 %collective-permute-start.17 = (bf16[2,288,128]{2,1,0:T(8,128)(2,1)S(1)}, bf16[2,288,128]{2,1,0:T(8,128)(2,1)S(1)}, u32[]{:S(2)}, u32[]{:S(2)}) collective-permute-start(bf16[2,288,128]{2,1,0:T(8,128)(2,1)S(1)} %join.1.refs_10_), channel_id=1, source_target_pairs={{0,6},{2,0},{4,2},{6,4},{1,7},{3,1},{5,3},{7,5},{8,14},{10,8},{12,... | collective-permute-start | bytes 442376 | tf_op jit(solution)/shard_map/ppermute | solution.py:27
  128.4 12.8 %collective-permute-start.11 = (bf16[4,288,128]{2,1,0:T(8,128)(2,1)S(1)}, bf16[4,288,128]{2,1,0:T(8,128)(2,1)S(1)}, u32[]{:S(2)}, u32[]{:S(2)}) collective-permute-start(bf16[4,288,128]{2,1,0:T(8,128)(2,1)S(1)} %rest.1.refs_2_), channel_id=1, source_target_pairs={{0,1},{1,0},{2,3},{3,2},{4,5},{5,4},{6,7},{7,6},{8,9},{9,8},{10,11... | collective-permute-start | bytes 884744 | tf_op jit(solution)/shard_map/ppermute | solution.py:27
  129.1 7.4 %collective-permute-start.16 = (bf16[2,288,128]{2,1,0:T(8,128)(2,1)S(1)}, bf16[2,288,128]{2,1,0:T(8,128)(2,1)S(1)}, u32[]{:S(2)}, u32[]{:S(2)}) collective-permute-start(bf16[2,288,128]{2,1,0:T(8,128)(2,1)S(1)} %join.1.refs_10_), channel_id=1, source_target_pairs={{0,4},{2,6},{4,0},{6,2},{1,5},{3,7},{5,1},{7,3},{8,12},{10,14},{12... | collective-permute-start | bytes 442376 | tf_op jit(solution)/shard_map/ppermute | solution.py:27
  134.8 6.4 %collective-permute-start.15 = (bf16[2,288,128]{2,1,0:T(8,128)(2,1)S(1)}, bf16[2,288,128]{2,1,0:T(8,128)(2,1)S(1)}, u32[]{:S(2)}, u32[]{:S(2)}) collective-permute-start(bf16[2,288,128]{2,1,0:T(8,128)(2,1)S(1)} %join.1.refs_10_), channel_id=1, source_target_pairs={{0,2},{2,4},{4,6},{6,0},{1,3},{3,5},{5,7},{7,1},{8,10},{10,12},{12... | collective-permute-start | bytes 442376 | tf_op jit(solution)/shard_map/ppermute | solution.py:27
  136.5 5.2 %collective-permute-start.21 = (bf16[2,288,128]{2,1,0:T(8,128)(2,1)S(1)}, bf16[2,288,128]{2,1,0:T(8,128)(2,1)S(1)}, u32[]{:S(2)}, u32[]{:S(2)}) collective-permute-start(bf16[2,288,128]{2,1,0:T(8,128)(2,1)S(1)} %collective-permute-done.17.refs_13_), channel_id=1, source_target_pairs={{0,1},{1,0},{2,3},{3,2},{4,5},{5,4},{6,7},{7,6},{8,9},{9,8},{10,11... | collective-permute-start | bytes 442376 | tf_op jit(solution)/shard_map/ppermute | solution.py:27
  141.1 3.4 %collective-permute-start.14 = (bf16[4,288,128]{2,1,0:T(8,128)(2,1)}, bf16[4,288,128]{2,1,0:T(8,128)(2,1)S(1)}, u32[]{:S(2)}, u32[]{:S(2)}) collective-permute-start(bf16[4,288,128]{2,1,0:T(8,128)(2,1)} %collective-permute-done.10.refs_5_), channel_id=1, source_target_pairs={{0,1},{1,0},{2,3},{3,2},{4,5},{5,4},{6,7},{7,6},{8,9},{9,8},{10,11... | collective-permute-start | bytes 884744 | tf_op jit(solution)/shard_map/ppermute | solution.py:27
  141.2 3.6 %collective-permute-start.13 = (bf16[4,288,128]{2,1,0:T(8,128)(2,1)S(1)}, bf16[4,288,128]{2,1,0:T(8,128)(2,1)S(1)}, u32[]{:S(2)}, u32[]{:S(2)}) collective-permute-start(bf16[4,288,128]{2,1,0:T(8,128)(2,1)S(1)} %collective-permute-done.9.refs_4_), channel_id=1, source_target_pairs={{0,1},{1,0},{2,3},{3,2},{4,5},{5,4},{6,7},{7,6},{8,9},{9,8},{10,11... | collective-permute-start | bytes 884744 | tf_op jit(solution)/shard_map/ppermute | solution.py:27
  141.7 3.4 %collective-permute-start.12 = (bf16[4,288,128]{2,1,0:T(8,128)(2,1)}, bf16[4,288,128]{2,1,0:T(8,128)(2,1)S(1)}, u32[]{:S(2)}, u32[]{:S(2)}) collective-permute-start(bf16[4,288,128]{2,1,0:T(8,128)(2,1)} %collective-permute-done.8.refs_3_), channel_id=1, source_target_pairs={{0,1},{1,0},{2,3},{3,2},{4,5},{5,4},{6,7},{7,6},{8,9},{9,8},{10,11... | collective-permute-start | bytes 884744 | tf_op jit(solution)/shard_map/ppermute | solution.py:27
  141.8 2.2 %collective-permute-start.20 = (bf16[2,288,128]{2,1,0:T(8,128)(2,1)S(1)}, bf16[2,288,128]{2,1,0:T(8,128)(2,1)S(1)}, u32[]{:S(2)}, u32[]{:S(2)}) collective-permute-start(bf16[2,288,128]{2,1,0:T(8,128)(2,1)S(1)} %collective-permute-done.16.refs_12_), channel_id=1, source_target_pairs={{0,1},{1,0},{2,3},{3,2},{4,5},{5,4},{6,7},{7,6},{8,9},{9,8},{10,11... | collective-permute-start | bytes 442376 | tf_op jit(solution)/shard_map/ppermute | solution.py:27
  142.2 2.0 %collective-permute-start.19 = (bf16[2,288,128]{2,1,0:T(8,128)(2,1)S(1)}, bf16[2,288,128]{2,1,0:T(8,128)(2,1)S(1)}, u32[]{:S(2)}, u32[]{:S(2)}) collective-permute-start(bf16[2,288,128]{2,1,0:T(8,128)(2,1)S(1)} %collective-permute-done.15.refs_11_), channel_id=1, source_target_pairs={{0,1},{1,0},{2,3},{3,2},{4,5},{5,4},{6,7},{7,6},{8,9},{9,8},{10,11... | collective-permute-start | bytes 442376 | tf_op jit(solution)/shard_map/ppermute | solution.py:27
  144.0 5.9 %collective-permute-start.37 = (bf16[2,144,1152]{2,1,0:T(8,128)(2,1)S(1)}, bf16[2,144,1152]{2,1,0:T(8,128)(2,1)S(1)}, u32[]{:S(2)}, u32[]{:S(2)}) collective-permute-start(bf16[2,144,1152]{2,1,0:T(8,128)(2,1)S(1)} %pack.1.refs_20_), channel_id=1, source_target_pairs={{0,1},{1,0},{2,3},{3,2},{4,5},{5,4},{6,7},{7,6},{8,9},{9,8},{10,11... | collective-permute-start | bytes 1990664 | tf_op jit(solution)/shard_map/ppermute | solution.py:27
  144.2 2.4 %collective-permute-start.44 = (bf16[144,1152]{1,0:T(8,128)(2,1)}, bf16[144,1152]{1,0:T(8,128)(2,1)S(1)}, u32[]{:S(2)}, u32[]{:S(2)}) collective-permute-start(bf16[144,1152]{1,0:T(8,128)(2,1)} %collective-permute-done.32.refs_27_), channel_id=1, source_target_pairs={{0,1},{1,0},{2,3},{3,2},{4,5},{5,4},{6,7},{7,6},{8,9},{9,8},{10,11... | collective-permute-start | bytes 995336 | tf_op jit(solution)/shard_map/ppermute | solution.py:27
  144.5 5.4 %collective-permute-start.42 = (bf16[2,144,1152]{2,1,0:T(8,128)(2,1)S(1)}, bf16[2,144,1152]{2,1,0:T(8,128)(2,1)S(1)}, u32[]{:S(2)}, u32[]{:S(2)}) collective-permute-start(bf16[2,144,1152]{2,1,0:T(8,128)(2,1)S(1)} %collective-permute-done.30.refs_25_), channel_id=1, source_target_pairs={{0,1},{1,0},{2,3},{3,2},{4,5},{5,4},{6,7},{7,6},{8,9},{9,8},{10,11... | collective-permute-start | bytes 1990664 | tf_op jit(solution)/shard_map/ppermute | solution.py:27
  144.7 5.2 %collective-permute-start.43 = (bf16[2,144,1152]{2,1,0:T(8,128)(2,1)S(1)}, bf16[2,144,1152]{2,1,0:T(8,128)(2,1)S(1)}, u32[]{:S(2)}, u32[]{:S(2)}) collective-permute-start(bf16[2,144,1152]{2,1,0:T(8,128)(2,1)S(1)} %collective-permute-done.31.refs_26_), channel_id=1, source_target_pairs={{0,1},{1,0},{2,3},{3,2},{4,5},{5,4},{6,7},{7,6},{8,9},{9,8},{10,11... | collective-permute-start | bytes 1990664 | tf_op jit(solution)/shard_map/ppermute | solution.py:27
  145.0 4.9 %collective-permute-start.46 = (bf16[2,144,1152]{2,1,0:T(8,128)(2,1)S(1)}, bf16[2,144,1152]{2,1,0:T(8,128)(2,1)S(1)}, u32[]{:S(2)}, u32[]{:S(2)}) collective-permute-start(bf16[2,144,1152]{2,1,0:T(8,128)(2,1)S(1)} %collective-permute-done.34.refs_29_), channel_id=1, source_target_pairs={{0,1},{1,0},{2,3},{3,2},{4,5},{5,4},{6,7},{7,6},{8,9},{9,8},{10,11... | collective-permute-start | bytes 1990664 | tf_op jit(solution)/shard_map/ppermute | solution.py:27
  146.6 3.3 %collective-permute-start.45 = (bf16[144,1152]{1,0:T(8,128)(2,1)}, bf16[144,1152]{1,0:T(8,128)(2,1)S(1)}, u32[]{:S(2)}, u32[]{:S(2)}) collective-permute-start(bf16[144,1152]{1,0:T(8,128)(2,1)} %collective-permute-done.33.refs_28_), channel_id=1, source_target_pairs={{0,1},{1,0},{2,3},{3,2},{4,5},{5,4},{6,7},{7,6},{8,9},{9,8},{10,11... | collective-permute-start | bytes 995336 | tf_op jit(solution)/shard_map/ppermute | solution.py:27
where the time goes:
time: 172 us; the launch traced here: 170 us
  waiting for transfers between devices  72.3 us (42%)
  starting transfers between devices  63.8 us (37%)
  Pallas kernels  32.4 us (19%)
    ppermute x45, starting transfers between devices, shift(): lax.ppermute(value, axis, [(i, (i + distance) % size) for i in range(size)])  43.1 us
    ppermute x45, waiting for transfers between devices, shift(): lax.ppermute(value, axis, [(i, (i + distance) % size) for i in range(size)])  42.3 us
    pallas_call x1, Pallas kernels, tail(): pl.pallas_call(functools.partial(tail_kernel, spots), out_shape=jax.Shape...  20.3 us
    ppermute x1, waiting for transfers between devices, layer(): partner = lax.ppermute(block, 'z', [(i, i ^ 1) for i in range(nz)])  20.1 us
    all_to_all x1, waiting for transfers between devices, layer(): before = lax.all_to_all(cuts, ('x', 'z'), 0, 0)  9.68 us
    all_to_all x1, starting transfers between devices, layer(): before = lax.all_to_all(cuts, ('x', 'z'), 0, 0)  8.87 us
    all_to_all x1, starting transfers between devices, layer(): cuts = lax.all_to_all(cuts, ('x', 'z'), 0, 0)  6 us
    pallas_call x1, Pallas kernels, local_kv(): pl.pallas_call(kv_kernel, out_shape=[jax.ShapeDtypeStruct((frames, HALF_R...  5.48 us
  transfers between devices with their start and end apart: 49, of which 19 were waited for; matrix products, arithmetic and copies ran while one was open for 0% of the time, Pallas kernels for 4%

commit v1 on v0

--- a/solution.py
+++ b/solution.py
@@ -18,17 +18,13 @@
 PAIR = 2 * PADDED
 CHUNK = 288
 HALF_COLS = 1152
-COL_TILE = 384
+COL_TILE = 256
 
 stab_eps = 1e-06
 
 
 def shift(value, axis, distance, size):
     return lax.ppermute(value, axis, [(i, (i + distance) % size) for i in range(size)])
-
-
-def next_section(value, size):
-    return lax.ppermute(value, ("x", "z"), [(i, i + 1) for i in range(size - 1)])
 
 
 def after(value, *others):
@@ -46,17 +42,22 @@
     tokens = k_ref.shape[2]
     pad = jnp.zeros((LANES - HEAD_DIM, tokens), jnp.bfloat16)
     ones = (lax.broadcasted_iota(jnp.int32, (LANES, tokens), 0) == HEAD_DIM).astype(jnp.bfloat16)
-    for head in range(HEADS):
-        half, inner = divmod(head, HALF_HEADS)
-        keys = jnp.maximum(k_ref[0, head * HEAD_DIM : (head + 1) * HEAD_DIM, :], 0)
-        vals = v_ref[0, head * HEAD_DIM : (head + 1) * HEAD_DIM, :]
-        left = jnp.concatenate([vals, keys], axis=1)
-        right = jnp.concatenate([jnp.concatenate([keys, pad], axis=0), ones], axis=1)
-        part = lax.dot_general(
-            left, right, (((1,), (1,)), ((), ())), preferred_element_type=jnp.float32
-        )
-        rows = slice(inner * HEAD_DIM, (inner + 1) * HEAD_DIM)
-        acc_ref[half, rows, :] = acc_ref[half, rows, :] + part
+
+    @pl.loop(0, 2)
+    def _(half):
+        for inner in range(HALF_HEADS):
+            start = half * (HALF_HEADS * HEAD_DIM) + inner * HEAD_DIM
+            rows = pl.ds(pl.multiple_of(start, 16), HEAD_DIM)
+            keys = jnp.maximum(k_ref[0, rows, :], 0)
+            vals = v_ref[0, rows, :]
+            left = jnp.concatenate([vals, keys], axis=1)
+            right = jnp.concatenate([jnp.concatenate([keys, pad], axis=0), ones], axis=1)
+            part = lax.dot_general(
+                left, right, (((1,), (1,)), ((), ())), preferred_element_type=jnp.float32
+            )
+            rows = slice(inner * HEAD_DIM, (inner + 1) * HEAD_DIM)
+            acc_ref[half, rows, :] = acc_ref[half, rows, :] + part
+
     norm = lax.broadcasted_iota(jnp.int32, (PADDED, LANES), 1) == HEAD_DIM
     for ref, half in ((mine_ref, core), (theirs_ref, 1 - core)):
         for pair in range(HALF_ROWS // PAIR):
@@ -91,23 +92,6 @@
         ),
         name="local_kv",
     )(core, keys, values)
-
-
-def copy_kernel(in_ref, out_ref):
-    out_ref[...] = in_ref[...]
-
-
-def last_two(queries):
-    frames, _, tokens = queries.shape
-    return pl.pallas_call(
-        copy_kernel,
-        out_shape=jax.ShapeDtypeStruct((2, D, tokens), queries.dtype),
-        grid=(4,),
-        in_specs=[pl.BlockSpec((1, D // 2, tokens), lambda i: (frames - 2 + i // 2, i % 2, 0))],
-        out_specs=pl.BlockSpec((1, D // 2, tokens), lambda i: (i // 2, i % 2, 0)),
-        compiler_params=limit(60),
-        name="last_two",
-    )(queries)
 
 
 def split_kernel(row_ref, mine_ref, other_ref, own_ref, *piece_refs):
@@ -289,7 +273,7 @@
     c_refs, p_refs = (refs[2:6], refs[6:10]), (refs[10:14], refs[14:18])
     count = len(spots)
     w_refs = (refs[18 : 18 + count], refs[18 + count : 18 + 2 * count])
-    taps_ref, out_ref, state_ref, att_ref, weight_ref, sem = refs[18 + 2 * count :]
+    taps_ref, out_ref, state_ref, query_ref, att_ref, weight_ref, sem = refs[18 + 2 * count :]
     step = pl.program_id(0)
     core, row = where_ref[0], where_ref[1]
     frames, width, tokens = out_ref.shape
@@ -314,63 +298,59 @@
         for copy in copies():
             copy.start()
 
-    def fill(before, within):
+    @pl.when(step < steps)
+    def _():
+        before = jnp.where(step == 0, 1, 0)
+        within = jnp.where(step >= 2, 1.0, 0.0)
         for which in range(2):
             half = which ^ core
             for s in range(4):
                 chunk = lax.rem(row - s + 4, 4)
-                state = p_refs[which][s][before]
-                if within:
-                    state = state.astype(jnp.float32) + c_refs[which][s][0].astype(jnp.float32)
+                state = p_refs[which][s][before].astype(jnp.float32)
+                state = state + c_refs[which][s][0].astype(jnp.float32) * within
                 start = pl.multiple_of(chunk * CHUNK, CHUNK)
                 state_ref[half, pl.ds(start, CHUNK), :] = state.astype(state_ref.dtype)
 
-    @pl.when(step == 0)
-    def _():
-        fill(1, False)
-
-    @pl.when(step == 1)
-    def _():
-        fill(0, False)
+    @pl.when(step < 2)
+    def _():
+        query_ref[...] = jnp.maximum(qh_ref[0], 0)
 
     @pl.when((step >= 2) & (step < steps))
     def _():
-        fill(0, True)
-
-    def heads(source):
+        query_ref[...] = jnp.maximum(q_ref[0], 0)
+
+    @pl.when(step < steps)
+    def _():
         pad = jnp.zeros((LANES - HEAD_DIM, tokens), jnp.bfloat16)
         lanes = pl.ds(pl.multiple_of(step * tokens, tokens), tokens)
-        for head in range(HEADS):
-            half, inner = divmod(head, HALF_HEADS)
-            query = jnp.maximum(source[0, head * HEAD_DIM : (head + 1) * HEAD_DIM, :], 0)
-            first = padded_row(inner * HEAD_DIM)
-            low = first // 16 * 16
-            high = -(-(padded_row(inner * HEAD_DIM + HEAD_DIM - 1) + 1) // 16) * 16
-            top = jnp.dot(
-                state_ref[half, low:high, :],
-                jnp.concatenate([query, pad], axis=0),
-                preferred_element_type=jnp.float32,
-            )
-            norm = state_ref[half, inner * HEAD_DIM : (inner + 1) * HEAD_DIM, HEAD_DIM : HEAD_DIM + 1]
-            bottom = norm.astype(jnp.float32) * query.astype(jnp.float32)
-            bottom = jnp.sum(bottom, axis=0, keepdims=True) + stab_eps
-            result = top * (1.0 / bottom)
-            base = half * HALF_ROWS
-            if first > low:
-                held = att_ref[base + low : base + low + 16, lanes].astype(jnp.float32)
-                keep = lax.broadcasted_iota(jnp.int32, (16, tokens), 0) < first - low
-                att_ref[base + low : base + low + 16, lanes] = jnp.where(keep, held, result[:16]).astype(att_ref.dtype)
-                att_ref[base + low + 16 : base + high, lanes] = result[16:].astype(att_ref.dtype)
-            else:
-                att_ref[base + low : base + high, lanes] = result.astype(att_ref.dtype)
-
-    @pl.when(step < 2)
-    def _():
-        heads(qh_ref)
-
-    @pl.when((step >= 2) & (step < steps))
-    def _():
-        heads(q_ref)
+
+        @pl.loop(0, 2)
+        def _(half):
+            for inner in range(HALF_HEADS):
+                start = half * (HALF_HEADS * HEAD_DIM) + inner * HEAD_DIM
+                query = query_ref[pl.ds(pl.multiple_of(start, 16), HEAD_DIM), :]
+                first = padded_row(inner * HEAD_DIM)
+                low = first // 16 * 16
+                high = -(-(padded_row(inner * HEAD_DIM + HEAD_DIM - 1) + 1) // 16) * 16
+                top = jnp.dot(
+                    state_ref[half, low:high, :],
+                    jnp.concatenate([query, pad], axis=0),
+                    preferred_element_type=jnp.float32,
+                )
+                norm = state_ref[half, inner * HEAD_DIM : (inner + 1) * HEAD_DIM, HEAD_DIM : HEAD_DIM + 1]
+                bottom = norm.astype(jnp.float32) * query.astype(jnp.float32)
+                bottom = jnp.sum(bottom, axis=0, keepdims=True) + stab_eps
+                result = top * (1.0 / bottom)
+                base = pl.multiple_of(half * HALF_ROWS + low, 16)
+                if first > low:
+                    edge = pl.ds(base, 16)
+                    held = att_ref[edge, lanes].astype(jnp.float32)
+                    keep = lax.broadcasted_iota(jnp.int32, (16, tokens), 0) < first - low
+                    att_ref[edge, lanes] = jnp.where(keep, held, result[:16]).astype(att_ref.dtype)
+                    inside = pl.ds(pl.multiple_of(base + 16, 16), high - low - 16)
+                    att_ref[inside, lanes] = result[16:].astype(att_ref.dtype)
+                else:
+                    att_ref[pl.ds(base, high - low), lanes] = result.astype(att_ref.dtype)
 
     @pl.when(step == steps)
     def _():
@@ -416,6 +396,7 @@
             out_specs=pl.BlockSpec((frames, COL_TILE, tokens), lambda f, w: (0, tile(f), 0)),
             scratch_shapes=[
                 pltpu.VMEM((2, HALF_ROWS, LANES), jnp.bfloat16),
+                pltpu.VMEM((D, tokens), jnp.bfloat16),
                 pltpu.VMEM((2 * HALF_ROWS, steps * tokens), jnp.bfloat16),
                 pltpu.VMEM((2 * HALF_ROWS, 2 * HALF_COLS), jnp.bfloat16),
                 pltpu.SemaphoreType.DMA((2 * pairs,)),
@@ -447,7 +428,10 @@
     padded = jnp.pad(out_weight, ((0, PADDED - rows), (0, 2 * HALF_COLS - cols)))
     block = lax.dynamic_slice_in_dim(padded, core * HALF_COLS, HALF_COLS, axis=1)
     partner = lax.ppermute(block, "z", [(i, i ^ 1) for i in range(nz)])
-    behind = next_section(last_two(queries), sections)
+    halo = queries[-2:]
+    over = lax.ppermute(
+        halo, ("x", "z"), [(i * nz + nz - 1, i * nz + 2 * nz - 1) for i in range(nx - 1)]
+    )
     mine, theirs = local_kv(jnp.reshape(core, (1,)), keys, values)
     theirs = shift(theirs, "c", 1, 2)
     pair = in_order(place, block, after(partner, mine))
@@ -461,35 +445,43 @@
 
     below = after(below, last)
     far = shift(below, "z", -2, nz)
-    below_up, below_down = shift(below, "x", 1, nx), shift(below, "x", -1, nx)
+    sides = pack([below, after(above, last)])
+    sides_up, sides_down = shift(sides, "x", 1, nx), shift(sides, "x", -1, nx)
     received = [shift(after(pieces[s + 2], last), "y", s, ny) for s in range(1, ny)]
     cuts = exclusive_scan(cuts)
     before = lax.all_to_all(cuts, ("x", "z"), 0, 0)
-    both = pack([after(above, cuts), after(far, cuts)])
-    both_up, both_down = shift(both, "x", 1, nx), shift(both, "x", -1, nx)
+    far_up, far_down = shift(after(far, cuts), "x", 1, nx), shift(after(far, cuts), "x", -1, nx)
+    sides_two = shift(after(sides_up, cuts), "x", 1, nx)
+    pair_two = shift(after(pair_down, cuts), "x", -1, nx)
+    halo = jnp.where(lax.axis_index("z") == nz - 1, after(over, cuts), halo)
+    behind = shift(halo, "z", 1, nz)
     sums = rest(own, [after(r, cuts) for r in received], last)
     c_mine = [sums] + along_y(sums)
-    pair_two = shift(after(pair_down, cuts), "x", -1, nx)
-    below_two = shift(after(below_down, cuts), "x", -1, nx)
-    early = to_partner([after(a, cuts) for a in (pair, below, both, pair_up, pair_down, below_up, below_down)])
+    early = to_partner([after(a, cuts) for a in (pair, pair_up, pair_down, sides)])
 
     before = join(before)
     p_mine = [before] + along_y(before)
-    both_two = shift(after(both_up, before), "x", 1, nx)
+    far_two = shift(after(far_down, before), "x", -1, nx)
     c_other = to_partner([after(a, before) for a in c_mine])
+    middle = to_partner([after(a, before) for a in (far, sides_up, sides_down, far_up, far_down)])
     p_other = to_partner(p_mine)
-    late = to_partner([after(a, before) for a in (both_up, both_down, pair_two, below_two, both_two)])
-
-    here, under, others = (0,), (-1,), (1, -2)
+    late = to_partner([after(a, before) for a in (pair_two, sides_two, far_two)])
+
+    here, near, across = (0,), (-1, 1), (-2,)
     spots = [
         [(dx, dz) for dz in steps]
         for dx, steps in (
-            (0, here), (0, under), (0, others), (1, here), (-1, here), (1, under), (-1, under),
-            (1, others), (-1, others), (-2, here), (-2, under), (2, others),
+            (0, here), (1, here), (-1, here), (0, near),
+            (0, across), (1, near), (-1, near), (1, across), (-1, across),
+            (-2, here), (2, near), (-2, across),
         )
     ]
-    groups = [pair, below, both, pair_up, pair_down, below_up, below_down, both_up, both_down, pair_two, below_two, both_two]
-    out = tail(where, behind, queries, c_mine, c_other, p_mine, p_other, groups, early + late, spots, conv_taps)
+    groups = [
+        pair, pair_up, pair_down, sides,
+        far, sides_up, sides_down, far_up, far_down,
+        pair_two, sides_two, far_two,
+    ]
+    out = tail(where, behind, queries, c_mine, c_other, p_mine, p_other, groups, early + middle + late, spots, conv_taps)
     return jnp.transpose(out, (0, 2, 1))
 
 

time: 172 us -> 177 us (1.029)
  starting transfers between devices: 63.8 us -> 59.9 us
  waiting for transfers between devices: 72.3 us -> 76.1 us
  local copies, waits for them, and re-layouts: 1.39 us -> 4.27 us
    ppermute x45 -> x46, waiting for transfers between devices: 42.3 us -> 60.3 us  [shift(): lax.ppermute(value, axis, [(i, (i + distance) % size) for i in range(size)])]
    ppermute x1, waiting for transfers between devices: 20.1 us -> 4.81 us  [layer(): partner = lax.ppermute(block, 'z', [(i, i ^ 1) for i in range(nz)])]
    pallas_call x1 -> x0, Pallas kernels: 3.52 us -> none  [last_two(): pl.pallas_call(copy_kernel, out_shape=jax.ShapeDtypeStruct((2, D, tokens)...]
    slice x0 -> x1, local copies, waits for them, and re-layouts: none -> 2.44 us  [layer(): halo = queries[-2:]]
    pallas_call x1, Pallas kernels: 20.3 us -> 22.6 us  [tail(): pl.pallas_call(functools.partial(tail_kernel, spots), out_shape=jax.Shape...]
    ppermute x1, starting transfers between devices: 3.82 us -> 1.67 us  [layer(): lax.ppermute(halo, ('x', 'z'), [(i * nz + nz - 1, i * nz + 2 * nz - 1) fo...]
    all_to_all x1, waiting for transfers between devices: 0.22 us -> 2.1 us  [layer(): cuts = lax.all_to_all(cuts, ('x', 'z'), 0, 0)]
    ppermute x45 -> x46, starting transfers between devices: 43.1 us -> 42.6 us  [shift(): lax.ppermute(value, axis, [(i, (i + distance) % size) for i in range(size)])]
  transfers between devices with their start and end apart: 49 -> 50, of which waited for: 19 -> 21; matrix products, arithmetic and copies ran while one was open for 0% -> 2% of each run, Pallas kernels for 4% -> 2%
where the time goes in v1:
time: 177 us; the launch traced here: 175 us
  waiting for transfers between devices  76.1 us (43%)
  starting transfers between devices  59.9 us (34%)
  Pallas kernels  32.9 us (19%)
  local copies, waits for them, and re-layouts  4.27 us (2%)
    ppermute x46, waiting for transfers between devices, shift(): lax.ppermute(value, axis, [(i, (i + distance) % size) for i in range(size)])  60.3 us
    ppermute x46, starting transfers between devices, shift(): lax.ppermute(value, axis, [(i, (i + distance) % size) for i in range(size)])  42.6 us
    pallas_call x1, Pallas kernels, tail(): pl.pallas_call(functools.partial(tail_kernel, spots), out_shape=jax.Shape...  22.6 us
    all_to_all x1, waiting for transfers between devices, layer(): before = lax.all_to_all(cuts, ('x', 'z'), 0, 0)  8.89 us
    all_to_all x1, starting transfers between devices, layer(): before = lax.all_to_all(cuts, ('x', 'z'), 0, 0)  7.77 us
    pallas_call x1, Pallas kernels, local_kv(): pl.pallas_call(kv_kernel, out_shape=[jax.ShapeDtypeStruct((frames, HALF_R...  6.09 us
    all_to_all x1, starting transfers between devices, layer(): cuts = lax.all_to_all(cuts, ('x', 'z'), 0, 0)  5.9 us
    ppermute x1, waiting for transfers between devices, layer(): partner = lax.ppermute(block, 'z', [(i, i ^ 1) for i in range(nz)])  4.81 us
  transfers between devices with their start and end apart: 50, of which 21 were waited for; matrix products, arithmetic and copies ran while one was open for 2% of the time, Pallas kernels for 2%

profile of v1, /device:TPU:2, one launch (start us, length us, event | category | flops | bytes accessed | tf_op | source)
XLA Modules:
  0.0 175.1 jit_solution(17652083562913631335)
XLA Ops:
  0.0 6.1 %local_kv.1 = (bf16[4,1152,128]{2,1,0:T(8,128)(2,1)}, bf16[4,1152,128]{2,1,0:T(8,128)(2,1)}) custom-call(s32[1]{0:T(128)} %bitcast.core_ref, bf16[4,2240,128]{2,1,0:T(8,128)(2,1)} %bitcast.8, bf16[4,2240,128]{2,1,0:T(8,128)(2,1)} %bitcast.9), custom_call_target="tpu_custom_call" | custom-call | flops 587202560 | bytes 9175040 | tf_op jit(solution)/shard_map/local_kv/pallas_call | solution.py:79
  6.1 2.4 %slice.4 = bf16[2,2240,128]{2,1,0:T(8,128)(2,1)} slice(bf16[4,2240,128]{2,1,0:T(8,128)(2,1)} %bitcast.10), slice={[2:4], [0:2240], [0:128]} | slice | bytes 2293760 | tf_op jit(solution)/shard_map/slice | solution.py:431
  8.6 1.7 collective-permute-start
  10.3 2.0 %collective-permute-start.23 = (bf16[72,1152]{1,0:T(8,128)(2,1)S(1)}, bf16[72,1152]{1,0:T(8,128)(2,1)S(1)}, u32[]{:S(2)}, u32[]{:S(2)}) collective-permute-start(bf16[72,1152]{1,0:T(8,128)(2,1)S(1)} %pad_dynamic-slice_fusion.mine_ref), channel_id=1, source_target_pairs={{0,8},{8,0},{16,24},{24,16},{32,40},{40,32},{48,56},{56,48},{1,9},... | collective-permute-start | bytes 497672 | tf_op jit(solution)/shard_map/ppermute | solution.py:430
  12.4 4.8 %collective-permute-done.23.other_ref = bf16[72,1152]{1,0:T(8,128)(2,1)S(1)} collective-permute-done((bf16[72,1152]{1,0:T(8,128)(2,1)S(1)}, bf16[72,1152]{1,0:T(8,128)(2,1)S(1)}, u32[]{:S(2)}, u32[]{:S(2)}) %collective-permute-start.23) | collective-permute-done | bytes 165920 | tf_op jit(solution)/shard_map/ppermute | solution.py:430
  17.2 0.6 in_order.1.refs_18_
  17.8 6.9 %collective-permute-start.26 = (bf16[144,1152]{1,0:T(8,128)(2,1)S(1)}, bf16[144,1152]{1,0:T(8,128)(2,1)}, u32[]{:S(2)}, u32[]{:S(2)}) collective-permute-start(bf16[144,1152]{1,0:T(8,128)(2,1)S(1)} %in_order.1.refs_18_), channel_id=1, source_target_pairs={{0,48},{8,56},{16,0},{24,8},{32,16},{40,24},{48,32},{56,40},{1,49}... | collective-permute-start | bytes 995336 | tf_op jit(solution)/shard_map/ppermute | solution.py:27
  24.7 0.8 split.1
  25.5 1.6 collective-permute-start.2
  27.1 2.9 %collective-permute-start.3 = (bf16[2,288,128]{2,1,0:T(8,128)(2,1)S(1)}, bf16[2,288,128]{2,1,0:T(8,128)(2,1)S(1)}, u32[]{:S(2)}, u32[]{:S(2)}) collective-permute-start(bf16[2,288,128]{2,1,0:T(8,128)(2,1)S(1)} %get-tuple-element.48), channel_id=1, source_target_pairs={{0,4},{2,6},{4,0},{6,2},{1,5},{3,7},{5,1},{7,3},{8,12},{10,14},{12... | collective-permute-start | bytes 442376 | tf_op jit(solution)/shard_map/ppermute | solution.py:27
  30.0 1.3 collective-permute-start.4
  31.3 1.0 collective-permute-done.2.a_ref
  32.3 3.9 %collective-permute-done.3.b_ref = bf16[2,288,128]{2,1,0:T(8,128)(2,1)S(1)} collective-permute-done((bf16[2,288,128]{2,1,0:T(8,128)(2,1)S(1)}, bf16[2,288,128]{2,1,0:T(8,128)(2,1)S(1)}, u32[]{:S(2)}, u32[]{:S(2)}) %collective-permute-start.3) | collective-permute-done | bytes 147488 | tf_op jit(solution)/shard_map/ppermute | solution.py:27
  36.2 0.8 total.1
  37.0 1.1 collective-permute-start.6
  38.1 2.7 %collective-permute-start.7 = (bf16[2,288,128]{2,1,0:T(8,128)(2,1)}, bf16[2,288,128]{2,1,0:T(8,128)(2,1)S(1)}, u32[]{:S(2)}, u32[]{:S(2)}) collective-permute-start(bf16[2,288,128]{2,1,0:T(8,128)(2,1)} %get-tuple-element.57), channel_id=1, source_target_pairs={{0,4},{2,6},{4,0},{6,2},{1,5},{3,7},{5,1},{7,3},{8,12},{10,14},{12... | collective-permute-start | bytes 442376 | tf_op jit(solution)/shard_map/ppermute | solution.py:27
  40.8 1.5 collective-permute-start.25
  42.4 2.6 %collective-permute-done.6.a_ref = bf16[2,288,128]{2,1,0:T(8,128)(2,1)S(1)} collective-permute-done((bf16[2,288,128]{2,1,0:T(8,128)(2,1)S(1)}, bf16[2,288,128]{2,1,0:T(8,128)(2,1)S(1)}, u32[]{:S(2)}, u32[]{:S(2)}) %collective-permute-start.6) | collective-permute-done | bytes 147488 | tf_op jit(solution)/shard_map/ppermute | solution.py:27
  44.9 1.2 collective-permute-start.24
  46.1 5.9 %all-to-all-start = ((bf16[32,18,128]{2,1,0:T(8,128)(2,1)}), bf16[32,18,128]{2,1,0:T(8,128)(2,1)S(1)}, u32[]{:S(2)}, u32[]{:S(2)}) async-start(bf16[32,18,128]{2,1,0:T(8,128)(2,1)} %get-tuple-element.50), calls=%async_computation | async-start | bytes 393216 | tf_op jit(solution)/shard_map/all_to_all | solution.py:444
  52.1 1.1 collective-permute-start.8
  53.1 4.2 %collective-permute-done.8.c_ref = bf16[2,288,128]{2,1,0:T(8,128)(2,1)S(1)} collective-permute-done((bf16[2,288,128]{2,1,0:T(8,128)(2,1)S(1)}, bf16[2,288,128]{2,1,0:T(8,128)(2,1)S(1)}, u32[]{:S(2)}, u32[]{:S(2)}) %collective-permute-start.8) | collective-permute-done | bytes 147488 | tf_op jit(solution)/shard_map/ppermute | solution.py:27
  57.3 3.6 %collective-permute-start.28 = (bf16[144,1152]{1,0:T(8,128)(2,1)}, bf16[144,1152]{1,0:T(8,128)(2,1)S(1)}, u32[]{:S(2)}, u32[]{:S(2)}) collective-permute-start(bf16[144,1152]{1,0:T(8,128)(2,1)} %collective-permute-done.26.refs_0_), channel_id=1, source_target_pairs={{0,48},{8,56},{16,0},{24,8},{32,16},{40,24},{48,32},{56,40},{1,49}... | collective-permute-start | bytes 995336 | tf_op jit(solution)/shard_map/ppermute | solution.py:27
  60.9 2.1 %all-to-all-done.in_ref = bf16[32,18,128]{2,1,0:T(8,128)(2,1)S(1)} async-done(((bf16[32,18,128]{2,1,0:T(8,128)(2,1)}), bf16[32,18,128]{2,1,0:T(8,128)(2,1)S(1)}, u32[]{:S(2)}, u32[]{:S(2)}) %all-to-all-start) | async-done | bytes 147488 | tf_op jit(solution)/shard_map/all_to_all | solution.py:444
  63.0 0.8 exclusive_scan.1
  63.8 0.6 collective-permute-start.11
  64.4 1.2 collective-permute-start.10
  65.6 0.5 collective-permute-start.9
  66.0 6.7 %collective-permute-done.28.refs_22_ = bf16[144,1152]{1,0:T(8,128)(2,1)S(1)} collective-permute-done((bf16[144,1152]{1,0:T(8,128)(2,1)}, bf16[144,1152]{1,0:T(8,128)(2,1)S(1)}, u32[]{:S(2)}, u32[]{:S(2)}) %collective-permute-start.28) | collective-permute-done | bytes 331808 | tf_op jit(solution)/shard_map/ppermute | solution.py:27
  72.7 0.6 collective-permute-start.33
  73.3 0.5 collective-permute-done.11.refs_5_
  73.8 1.1 pack.1.refs_21_
  74.9 1.0 collective-permute-done.10.refs_4_
  75.9 1.8 %collective-permute-start.30 = (bf16[2,144,1152]{2,1,0:T(8,128)(2,1)S(1)}, bf16[2,144,1152]{2,1,0:T(8,128)(2,1)S(1)}, u32[]{:S(2)}, u32[]{:S(2)}) collective-permute-start(bf16[2,144,1152]{2,1,0:T(8,128)(2,1)S(1)} %pack.1.refs_21_), channel_id=1, source_target_pairs={{0,192},{64,0},{128,64},{192,128},{1,193},{65,1},{129,65},{193,129... | collective-permute-start | bytes 1990664 | tf_op jit(solution)/shard_map/ppermute | solution.py:27
  77.7 2.3 %collective-permute-done.9.refs_3_ = bf16[4,288,128]{2,1,0:T(8,128)(2,1)} collective-permute-done((bf16[4,288,128]{2,1,0:T(8,128)(2,1)S(1)}, bf16[4,288,128]{2,1,0:T(8,128)(2,1)}, u32[]{:S(2)}, u32[]{:S(2)}) %collective-permute-start.9) | collective-permute-done | bytes 294944 | tf_op jit(solution)/shard_map/ppermute | solution.py:27
  80.0 1.4 collective-permute-start.29
  81.4 0.7 copy-done.5
  82.1 7.8 %all-to-all-start.1 = ((bf16[32,18,128]{2,1,0:T(8,128)(2,1)}), bf16[32,18,128]{2,1,0:T(8,128)(2,1)S(1)}, u32[]{:S(2)}, u32[]{:S(2)}) async-start(bf16[32,18,128]{2,1,0:T(8,128)(2,1)} %exclusive_scan.1), calls=%async_computation.1 | async-start | bytes 393216 | tf_op jit(solution)/shard_map/all_to_all | solution.py:452
  89.9 0.3 collective-permute-start.32
  90.3 1.8 %collective-permute-start.31 = (bf16[144,1152]{1,0:T(8,128)(2,1)}, bf16[144,1152]{1,0:T(8,128)(2,1)}, u32[]{:S(2)}, u32[]{:S(2)}) collective-permute-start(bf16[144,1152]{1,0:T(8,128)(2,1)} %copy-done.3), channel_id=1, source_target_pairs={{0,64},{64,128},{128,192},{192,0},{1,65},{65,129},{129,193},{193,1... | collective-permute-start | bytes 995336 | tf_op jit(solution)/shard_map/ppermute | solution.py:27
  92.0 8.9 %all-to-all-done.1.in_ref = bf16[32,18,128]{2,1,0:T(8,128)(2,1)S(1)} async-done(((bf16[32,18,128]{2,1,0:T(8,128)(2,1)}), bf16[32,18,128]{2,1,0:T(8,128)(2,1)S(1)}, u32[]{:S(2)}, u32[]{:S(2)}) %all-to-all-start.1) | async-done | bytes 147488 | tf_op jit(solution)/shard_map/all_to_all | solution.py:452
  101.1 4.3 %collective-permute-done.32.refs_26_ = bf16[144,1152]{1,0:T(8,128)(2,1)} collective-permute-done((bf16[144,1152]{1,0:T(8,128)(2,1)}, bf16[144,1152]{1,0:T(8,128)(2,1)}, u32[]{:S(2)}, u32[]{:S(2)}) %collective-permute-start.32) | collective-permute-done | bytes 331808 | tf_op jit(solution)/shard_map/ppermute | solution.py:27
  105.4 0.7 collective-permute-done.31.refs_25_
  106.1 1.3 collective-permute-start.18
  107.4 1.3 collective-permute-start.16
  108.8 5.6 %collective-permute-done.18.refs_13_ = bf16[2,288,128]{2,1,0:T(8,128)(2,1)S(1)} collective-permute-done((bf16[2,288,128]{2,1,0:T(8,128)(2,1)S(1)}, bf16[2,288,128]{2,1,0:T(8,128)(2,1)S(1)}, u32[]{:S(2)}, u32[]{:S(2)}) %collective-permute-start.18) | collective-permute-done | bytes 147488 | tf_op jit(solution)/shard_map/ppermute | solution.py:27
  114.4 1.3 collective-permute-done.17.refs_12_
  115.7 2.3 %collective-permute-done.16.refs_11_ = bf16[2,288,128]{2,1,0:T(8,128)(2,1)} collective-permute-done((bf16[2,288,128]{2,1,0:T(8,128)(2,1)S(1)}, bf16[2,288,128]{2,1,0:T(8,128)(2,1)}, u32[]{:S(2)}, u32[]{:S(2)}) %collective-permute-start.16) | collective-permute-done | bytes 147488 | tf_op jit(solution)/shard_map/ppermute | solution.py:27
  118.0 0.8 collective-permute-start.39
  118.9 0.4 collective-permute-start.14
  119.3 0.3 collective-permute-done.20.refs_15_
  119.8 1.5 collective-permute-start.34
  121.3 1.4 broadcast_select_fusion
  122.8 0.2 collective-permute-start.45
  123.0 0.4 collective-permute-start.44
  123.4 13.6 %collective-permute-done.34.refs_28_ = bf16[2,144,1152]{2,1,0:T(8,128)(2,1)S(1)} collective-permute-done((bf16[2,144,1152]{2,1,0:T(8,128)(2,1)S(1)}, bf16[2,144,1152]{2,1,0:T(8,128)(2,1)S(1)}, u32[]{:S(2)}, u32[]{:S(2)}) %collective-permute-start.34) | collective-permute-done | bytes 663584 | tf_op jit(solution)/shard_map/ppermute | solution.py:27
  137.0 3.1 %collective-permute-start.35 = (bf16[144,1152]{1,0:T(8,128)(2,1)}, bf16[144,1152]{1,0:T(8,128)(2,1)S(1)}, u32[]{:S(2)}, u32[]{:S(2)}) collective-permute-start(bf16[144,1152]{1,0:T(8,128)(2,1)} %collective-permute-done.32.refs_26_), channel_id=1, source_target_pairs={{0,192},{64,0},{128,64},{192,128},{1,193},{65,1},{129,65},{193,129... | collective-permute-start | bytes 995336 | tf_op jit(solution)/shard_map/ppermute | solution.py:27
  140.1 0.5 collective-permute-start.42
  140.7 6.7 %collective-permute-done.35.refs_29_ = bf16[144,1152]{1,0:T(8,128)(2,1)S(1)} collective-permute-done((bf16[144,1152]{1,0:T(8,128)(2,1)}, bf16[144,1152]{1,0:T(8,128)(2,1)S(1)}, u32[]{:S(2)}, u32[]{:S(2)}) %collective-permute-start.35) | collective-permute-done | bytes 331808 | tf_op jit(solution)/shard_map/ppermute | solution.py:27
  147.4 0.5 collective-permute-start.47
  148.0 2.0 %collective-permute-done.47.refs_41_ = bf16[144,1152]{1,0:T(8,128)(2,1)S(1)} collective-permute-done((bf16[144,1152]{1,0:T(8,128)(2,1)S(1)}, bf16[144,1152]{1,0:T(8,128)(2,1)S(1)}, u32[]{:S(2)}, u32[]{:S(2)}) %collective-permute-start.47) | collective-permute-done | bytes 331808 | tf_op jit(solution)/shard_map/ppermute | solution.py:27
  150.0 1.3 collective-permute-done.5.refs_0_
  151.3 1.0 copy-done.11
  152.3 22.6 %tail.1 = bf16[4,2240,128]{2,1,0:T(8,128)(2,1)} custom-call(s32[4]{0:T(128)S(1)} %pad_add_fusion.where_ref, bf16[2,2240,128]{2,1,0:T(8,128)(2,1)} %copy-done.11, bf16[4,2240,128]{2,1,0:T(8,128)(2,1)} %bitcast.12, bf16[4,288,128]{2,1,0:T(8,128)(2,1)S(1)} %rest.1.refs_2_, bf16[4,288,128]{2,1,0:T(8,128)(2,1)} %collective-permute-done.9.refs_3_, ...), custom_call_target="tpu_custom_call" | custom-call | flops 8147435520 | bytes 10035200 | tf_op jit(solution)/shard_map/tail/pallas_call | solution.py:382
  (74 shorter events, 1.0 us)
Async XLA Ops:
  6.1 4.1 %copy-start.10 = (bf16[70,2240]{1,0:T(8,128)(2,1)S(1)}, bf16[70,2240]{1,0:T(8,128)(2,1)}, u32[]{:S(2)}) copy-start(bf16[70,2240]{1,0:T(8,128)(2,1)} %param.8) | copy-start | bytes 940804
  6.1 18.6 %collective-permute-start.1 = (bf16[4,1152,128]{2,1,0:T(8,128)(2,1)}, bf16[4,1152,128]{2,1,0:T(8,128)(2,1)S(1)}, u32[]{:S(2)}, u32[]{:S(2)}) collective-permute-start(bf16[4,1152,128]{2,1,0:T(8,128)(2,1)} %get-tuple-element.45), channel_id=1, source_target_pairs={{0,1},{1,0},{2,3},{3,2},{4,5},{5,4},{6,7},{7,6},{8,9},{9,8},{10,11... | collective-permute-start | bytes 3538952 | tf_op jit(solution)/shard_map/ppermute | solution.py:27
  6.1 18.6 %copy-start = (bf16[4,1152,128]{2,1,0:T(8,128)(2,1)S(1)}, bf16[4,1152,128]{2,1,0:T(8,128)(2,1)}, u32[]{:S(2)}) copy-start(bf16[4,1152,128]{2,1,0:T(8,128)(2,1)} %get-tuple-element.44.mine_ref) | copy-start | bytes 3538948
  8.6 57.5 %collective-permute-start = (bf16[2,2240,128]{2,1,0:T(8,128)(2,1)}, bf16[2,2240,128]{2,1,0:T(8,128)(2,1)}, u32[]{:S(2)}, u32[]{:S(2)}) collective-permute-start(bf16[2,2240,128]{2,1,0:T(8,128)(2,1)} %slice.4), channel_id=1, source_target_pairs={{56,120},{120,184},{184,248},{57,121},{121,185},{185,249},{58,122}... | collective-permute-start | bytes 3440648 | tf_op jit(solution)/shard_map/ppermute | solution.py:432
  10.3 6.9 %collective-permute-start.23 = (bf16[72,1152]{1,0:T(8,128)(2,1)S(1)}, bf16[72,1152]{1,0:T(8,128)(2,1)S(1)}, u32[]{:S(2)}, u32[]{:S(2)}) collective-permute-start(bf16[72,1152]{1,0:T(8,128)(2,1)S(1)} %pad_dynamic-slice_fusion.mine_ref), channel_id=1, source_target_pairs={{0,8},{8,0},{16,24},{24,16},{32,40},{40,32},{48,56},{56,48},{1,9},... | collective-permute-start | bytes 497672 | tf_op jit(solution)/shard_map/ppermute | solution.py:430
  17.8 23.1 %collective-permute-start.26 = (bf16[144,1152]{1,0:T(8,128)(2,1)S(1)}, bf16[144,1152]{1,0:T(8,128)(2,1)}, u32[]{:S(2)}, u32[]{:S(2)}) collective-permute-start(bf16[144,1152]{1,0:T(8,128)(2,1)S(1)} %in_order.1.refs_18_), channel_id=1, source_target_pairs={{0,48},{8,56},{16,0},{24,8},{32,16},{40,24},{48,32},{56,40},{1,49}... | collective-permute-start | bytes 995336 | tf_op jit(solution)/shard_map/ppermute | solution.py:27
  25.5 6.8 %collective-permute-start.2 = (bf16[2,288,128]{2,1,0:T(8,128)(2,1)S(1)}, bf16[2,288,128]{2,1,0:T(8,128)(2,1)S(1)}, u32[]{:S(2)}, u32[]{:S(2)}) collective-permute-start(bf16[2,288,128]{2,1,0:T(8,128)(2,1)S(1)} %get-tuple-element.47), channel_id=1, source_target_pairs={{0,2},{2,4},{4,6},{6,0},{1,3},{3,5},{5,7},{7,1},{8,10},{10,12},{12... | collective-permute-start | bytes 442376 | tf_op jit(solution)/shard_map/ppermute | solution.py:27
  27.1 9.1 %collective-permute-start.3 = (bf16[2,288,128]{2,1,0:T(8,128)(2,1)S(1)}, bf16[2,288,128]{2,1,0:T(8,128)(2,1)S(1)}, u32[]{:S(2)}, u32[]{:S(2)}) collective-permute-start(bf16[2,288,128]{2,1,0:T(8,128)(2,1)S(1)} %get-tuple-element.48), channel_id=1, source_target_pairs={{0,4},{2,6},{4,0},{6,2},{1,5},{3,7},{5,1},{7,3},{8,12},{10,14},{12... | collective-permute-start | bytes 442376 | tf_op jit(solution)/shard_map/ppermute | solution.py:27
  30.0 6.2 %collective-permute-start.4 = (bf16[2,288,128]{2,1,0:T(8,128)(2,1)S(1)}, bf16[2,288,128]{2,1,0:T(8,128)(2,1)S(1)}, u32[]{:S(2)}, u32[]{:S(2)}) collective-permute-start(bf16[2,288,128]{2,1,0:T(8,128)(2,1)S(1)} %get-tuple-element.49), channel_id=1, source_target_pairs={{0,6},{2,0},{4,2},{6,4},{1,7},{3,1},{5,3},{7,5},{8,14},{10,8},{12,... | collective-permute-start | bytes 442376 | tf_op jit(solution)/shard_map/ppermute | solution.py:27
  37.0 7.9 %collective-permute-start.6 = (bf16[2,288,128]{2,1,0:T(8,128)(2,1)S(1)}, bf16[2,288,128]{2,1,0:T(8,128)(2,1)S(1)}, u32[]{:S(2)}, u32[]{:S(2)}) collective-permute-start(bf16[2,288,128]{2,1,0:T(8,128)(2,1)S(1)} %get-tuple-element.54), channel_id=1, source_target_pairs={{0,2},{2,4},{4,6},{6,0},{1,3},{3,5},{5,7},{7,1},{8,10},{10,12},{12... | collective-permute-start | bytes 442376 | tf_op jit(solution)/shard_map/ppermute | solution.py:27
  38.1 13.9 %collective-permute-start.7 = (bf16[2,288,128]{2,1,0:T(8,128)(2,1)}, bf16[2,288,128]{2,1,0:T(8,128)(2,1)S(1)}, u32[]{:S(2)}, u32[]{:S(2)}) collective-permute-start(bf16[2,288,128]{2,1,0:T(8,128)(2,1)} %get-tuple-element.57), channel_id=1, source_target_pairs={{0,4},{2,6},{4,0},{6,2},{1,5},{3,7},{5,1},{7,3},{8,12},{10,14},{12... | collective-permute-start | bytes 442376 | tf_op jit(solution)/shard_map/ppermute | solution.py:27
  40.8 23.0 %collective-permute-start.27 = (bf16[144,1152]{1,0:T(8,128)(2,1)S(1)}, bf16[144,1152]{1,0:T(8,128)(2,1)S(1)}, u32[]{:S(2)}, u32[]{:S(2)}) collective-permute-start(bf16[144,1152]{1,0:T(8,128)(2,1)S(1)} %in_order.1.refs_18_), channel_id=1, source_target_pairs={{0,16},{8,24},{16,32},{24,40},{32,48},{40,56},{48,0},{56,8},{1,17}... | collective-permute-start | bytes 995336 | tf_op jit(solution)/shard_map/ppermute | solution.py:27
  40.8 23.6 %collective-permute-start.25 = (bf16[144,1152]{1,0:T(8,128)(2,1)S(1)}, bf16[144,1152]{1,0:T(8,128)(2,1)}, u32[]{:S(2)}, u32[]{:S(2)}) collective-permute-start(bf16[144,1152]{1,0:T(8,128)(2,1)S(1)} %in_order.1.refs_18_), channel_id=1, source_target_pairs={{0,192},{64,0},{128,64},{192,128},{1,193},{65,1},{129,65},{193,129... | collective-permute-start | bytes 995336 | tf_op jit(solution)/shard_map/ppermute | solution.py:27
  44.9 20.6 %collective-permute-start.24 = (bf16[144,1152]{1,0:T(8,128)(2,1)S(1)}, bf16[144,1152]{1,0:T(8,128)(2,1)S(1)}, u32[]{:S(2)}, u32[]{:S(2)}) collective-permute-start(bf16[144,1152]{1,0:T(8,128)(2,1)S(1)} %in_order.1.refs_18_), channel_id=1, source_target_pairs={{0,64},{64,128},{128,192},{192,0},{1,65},{65,129},{129,193},{193,1... | collective-permute-start | bytes 995336 | tf_op jit(solution)/shard_map/ppermute | solution.py:27
  46.1 16.8 %all-to-all-start = ((bf16[32,18,128]{2,1,0:T(8,128)(2,1)}), bf16[32,18,128]{2,1,0:T(8,128)(2,1)S(1)}, u32[]{:S(2)}, u32[]{:S(2)}) async-start(bf16[32,18,128]{2,1,0:T(8,128)(2,1)} %get-tuple-element.50), calls=%async_computation | async-start | bytes 393216 | tf_op jit(solution)/shard_map/all_to_all | solution.py:444
  52.1 5.2 %collective-permute-start.8 = (bf16[2,288,128]{2,1,0:T(8,128)(2,1)S(1)}, bf16[2,288,128]{2,1,0:T(8,128)(2,1)S(1)}, u32[]{:S(2)}, u32[]{:S(2)}) collective-permute-start(bf16[2,288,128]{2,1,0:T(8,128)(2,1)S(1)} %get-tuple-element.60), channel_id=1, source_target_pairs={{0,6},{2,0},{4,2},{6,4},{1,7},{3,1},{5,3},{7,5},{8,14},{10,8},{12,... | collective-permute-start | bytes 442376 | tf_op jit(solution)/shard_map/ppermute | solution.py:27
  57.3 15.4 %collective-permute-start.28 = (bf16[144,1152]{1,0:T(8,128)(2,1)}, bf16[144,1152]{1,0:T(8,128)(2,1)S(1)}, u32[]{:S(2)}, u32[]{:S(2)}) collective-permute-start(bf16[144,1152]{1,0:T(8,128)(2,1)} %collective-permute-done.26.refs_0_), channel_id=1, source_target_pairs={{0,48},{8,56},{16,0},{24,8},{32,16},{40,24},{48,32},{56,40},{1,49}... | collective-permute-start | bytes 995336 | tf_op jit(solution)/shard_map/ppermute | solution.py:27
  63.8 10.0 %collective-permute-start.11 = (bf16[4,288,128]{2,1,0:T(8,128)(2,1)S(1)}, bf16[4,288,128]{2,1,0:T(8,128)(2,1)S(1)}, u32[]{:S(2)}, u32[]{:S(2)}) collective-permute-start(bf16[4,288,128]{2,1,0:T(8,128)(2,1)S(1)} %rest.1.refs_2_), channel_id=1, source_target_pairs={{0,6},{2,0},{4,2},{6,4},{1,7},{3,1},{5,3},{7,5},{8,14},{10,8},{12,... | collective-permute-start | bytes 884744 | tf_op jit(solution)/shard_map/ppermute | solution.py:27
  64.4 11.5 %collective-permute-start.10 = (bf16[4,288,128]{2,1,0:T(8,128)(2,1)S(1)}, bf16[4,288,128]{2,1,0:T(8,128)(2,1)}, u32[]{:S(2)}, u32[]{:S(2)}) collective-permute-start(bf16[4,288,128]{2,1,0:T(8,128)(2,1)S(1)} %rest.1.refs_2_), channel_id=1, source_target_pairs={{0,4},{2,6},{4,0},{6,2},{1,5},{3,7},{5,1},{7,3},{8,12},{10,14},{12... | collective-permute-start | bytes 884744 | tf_op jit(solution)/shard_map/ppermute | solution.py:27
  65.6 9.4 %copy-start.1 = (bf16[144,1152]{1,0:T(8,128)(2,1)}, bf16[144,1152]{1,0:T(8,128)(2,1)S(1)}, u32[]{:S(2)}) copy-start(bf16[144,1152]{1,0:T(8,128)(2,1)S(1)} %collective-permute-done.24.refs_19_) | copy-start | bytes 995332
  65.6 14.4 %collective-permute-start.9 = (bf16[4,288,128]{2,1,0:T(8,128)(2,1)S(1)}, bf16[4,288,128]{2,1,0:T(8,128)(2,1)}, u32[]{:S(2)}, u32[]{:S(2)}) collective-permute-start(bf16[4,288,128]{2,1,0:T(8,128)(2,1)S(1)} %rest.1.refs_2_), channel_id=1, source_target_pairs={{0,2},{2,4},{4,6},{6,0},{1,3},{3,5},{5,7},{7,1},{8,10},{10,12},{12... | collective-permute-start | bytes 884744 | tf_op jit(solution)/shard_map/ppermute | solution.py:27
  66.0 15.4 %collective-permute-start.38 = (bf16[144,1152]{1,0:T(8,128)(2,1)}, bf16[144,1152]{1,0:T(8,128)(2,1)S(1)}, u32[]{:S(2)}, u32[]{:S(2)}) collective-permute-start(bf16[144,1152]{1,0:T(8,128)(2,1)} %collective-permute-done.25.refs_20_), channel_id=1, source_target_pairs={{0,1},{1,0},{2,3},{3,2},{4,5},{5,4},{6,7},{7,6},{8,9},{9,8},{10,11... | collective-permute-start | bytes 995336 | tf_op jit(solution)/shard_map/ppermute | solution.py:27
  72.7 5.0 %copy-start.3 = (bf16[144,1152]{1,0:T(8,128)(2,1)}, bf16[144,1152]{1,0:T(8,128)(2,1)S(1)}, u32[]{:S(2)}) copy-start(bf16[144,1152]{1,0:T(8,128)(2,1)S(1)} %collective-permute-done.28.refs_22_) | copy-start | bytes 995332
  72.7 17.2 %collective-permute-start.33 = (bf16[144,1152]{1,0:T(8,128)(2,1)}, bf16[144,1152]{1,0:T(8,128)(2,1)}, u32[]{:S(2)}, u32[]{:S(2)}) collective-permute-start(bf16[144,1152]{1,0:T(8,128)(2,1)} %collective-permute-done.25.refs_20_), channel_id=1, source_target_pairs={{0,192},{64,0},{128,64},{192,128},{1,193},{65,1},{129,65},{193,129... | collective-permute-start | bytes 995336 | tf_op jit(solution)/shard_map/ppermute | solution.py:27
  73.8 1.2 copy-start.7
  73.8 16.5 %collective-permute-start.36 = (bf16[144,1152]{1,0:T(8,128)(2,1)S(1)}, bf16[144,1152]{1,0:T(8,128)(2,1)}, u32[]{:S(2)}, u32[]{:S(2)}) collective-permute-start(bf16[144,1152]{1,0:T(8,128)(2,1)S(1)} %in_order.1.refs_18_), channel_id=1, source_target_pairs={{0,1},{1,0},{2,3},{3,2},{4,5},{5,4},{6,7},{7,6},{8,9},{9,8},{10,11... | collective-permute-start | bytes 995336 | tf_op jit(solution)/shard_map/ppermute | solution.py:27
  75.9 31.5 %collective-permute-start.30 = (bf16[2,144,1152]{2,1,0:T(8,128)(2,1)S(1)}, bf16[2,144,1152]{2,1,0:T(8,128)(2,1)S(1)}, u32[]{:S(2)}, u32[]{:S(2)}) collective-permute-start(bf16[2,144,1152]{2,1,0:T(8,128)(2,1)S(1)} %pack.1.refs_21_), channel_id=1, source_target_pairs={{0,192},{64,0},{128,64},{192,128},{1,193},{65,1},{129,65},{193,129... | collective-permute-start | bytes 1990664 | tf_op jit(solution)/shard_map/ppermute | solution.py:27
  80.0 27.4 %collective-permute-start.29 = (bf16[2,144,1152]{2,1,0:T(8,128)(2,1)S(1)}, bf16[2,144,1152]{2,1,0:T(8,128)(2,1)S(1)}, u32[]{:S(2)}, u32[]{:S(2)}) collective-permute-start(bf16[2,144,1152]{2,1,0:T(8,128)(2,1)S(1)} %pack.1.refs_21_), channel_id=1, source_target_pairs={{0,64},{64,128},{128,192},{192,0},{1,65},{65,129},{129,193},{193,1... | collective-permute-start | bytes 1990664 | tf_op jit(solution)/shard_map/ppermute | solution.py:27
  81.4 0.7 copy-start.5
  82.1 18.9 %collective-permute-start.37 = (bf16[144,1152]{1,0:T(8,128)(2,1)}, bf16[144,1152]{1,0:T(8,128)(2,1)}, u32[]{:S(2)}, u32[]{:S(2)}) collective-permute-start(bf16[144,1152]{1,0:T(8,128)(2,1)} %copy-done.1), channel_id=1, source_target_pairs={{0,1},{1,0},{2,3},{3,2},{4,5},{5,4},{6,7},{7,6},{8,9},{9,8},{10,11... | collective-permute-start | bytes 995336 | tf_op jit(solution)/shard_map/ppermute | solution.py:27
  82.1 18.8 %all-to-all-start.1 = ((bf16[32,18,128]{2,1,0:T(8,128)(2,1)}), bf16[32,18,128]{2,1,0:T(8,128)(2,1)S(1)}, u32[]{:S(2)}, u32[]{:S(2)}) async-start(bf16[32,18,128]{2,1,0:T(8,128)(2,1)} %exclusive_scan.1), calls=%async_computation.1 | async-start | bytes 393216 | tf_op jit(solution)/shard_map/all_to_all | solution.py:452
  89.9 15.5 %collective-permute-start.32 = (bf16[144,1152]{1,0:T(8,128)(2,1)}, bf16[144,1152]{1,0:T(8,128)(2,1)}, u32[]{:S(2)}, u32[]{:S(2)}) collective-permute-start(bf16[144,1152]{1,0:T(8,128)(2,1)} %copy-done.3), channel_id=1, source_target_pairs={{0,192},{64,0},{128,64},{192,128},{1,193},{65,1},{129,65},{193,129... | collective-permute-start | bytes 995336 | tf_op jit(solution)/shard_map/ppermute | solution.py:27
  90.3 15.9 %collective-permute-start.31 = (bf16[144,1152]{1,0:T(8,128)(2,1)}, bf16[144,1152]{1,0:T(8,128)(2,1)}, u32[]{:S(2)}, u32[]{:S(2)}) collective-permute-start(bf16[144,1152]{1,0:T(8,128)(2,1)} %copy-done.3), channel_id=1, source_target_pairs={{0,64},{64,128},{128,192},{192,0},{1,65},{65,129},{129,193},{193,1... | collective-permute-start | bytes 995336 | tf_op jit(solution)/shard_map/ppermute | solution.py:27
  101.0 7.7 %collective-permute-start.19 = (bf16[2,288,128]{2,1,0:T(8,128)(2,1)S(1)}, bf16[2,288,128]{2,1,0:T(8,128)(2,1)S(1)}, u32[]{:S(2)}, u32[]{:S(2)}) collective-permute-start(bf16[2,288,128]{2,1,0:T(8,128)(2,1)S(1)} %join.1.refs_10_), channel_id=1, source_target_pairs={{0,1},{1,0},{2,3},{3,2},{4,5},{5,4},{6,7},{7,6},{8,9},{9,8},{10,11... | collective-permute-start | bytes 442376 | tf_op jit(solution)/shard_map/ppermute | solution.py:27
  105.4 12.6 %collective-permute-start.12 = (bf16[4,288,128]{2,1,0:T(8,128)(2,1)S(1)}, bf16[4,288,128]{2,1,0:T(8,128)(2,1)}, u32[]{:S(2)}, u32[]{:S(2)}) collective-permute-start(bf16[4,288,128]{2,1,0:T(8,128)(2,1)S(1)} %rest.1.refs_2_), channel_id=1, source_target_pairs={{0,1},{1,0},{2,3},{3,2},{4,5},{5,4},{6,7},{7,6},{8,9},{9,8},{10,11... | collective-permute-start | bytes 884744 | tf_op jit(solution)/shard_map/ppermute | solution.py:27
  106.1 8.3 %collective-permute-start.18 = (bf16[2,288,128]{2,1,0:T(8,128)(2,1)S(1)}, bf16[2,288,128]{2,1,0:T(8,128)(2,1)S(1)}, u32[]{:S(2)}, u32[]{:S(2)}) collective-permute-start(bf16[2,288,128]{2,1,0:T(8,128)(2,1)S(1)} %join.1.refs_10_), channel_id=1, source_target_pairs={{0,6},{2,0},{4,2},{6,4},{1,7},{3,1},{5,3},{7,5},{8,14},{10,8},{12,... | collective-permute-start | bytes 442376 | tf_op jit(solution)/shard_map/ppermute | solution.py:27
  107.4 8.3 %collective-permute-start.17 = (bf16[2,288,128]{2,1,0:T(8,128)(2,1)S(1)}, bf16[2,288,128]{2,1,0:T(8,128)(2,1)S(1)}, u32[]{:S(2)}, u32[]{:S(2)}) collective-permute-start(bf16[2,288,128]{2,1,0:T(8,128)(2,1)S(1)} %join.1.refs_10_), channel_id=1, source_target_pairs={{0,4},{2,6},{4,0},{6,2},{1,5},{3,7},{5,1},{7,3},{8,12},{10,14},{12... | collective-permute-start | bytes 442376 | tf_op jit(solution)/shard_map/ppermute | solution.py:27
  107.4 10.5 %collective-permute-start.16 = (bf16[2,288,128]{2,1,0:T(8,128)(2,1)S(1)}, bf16[2,288,128]{2,1,0:T(8,128)(2,1)}, u32[]{:S(2)}, u32[]{:S(2)}) collective-permute-start(bf16[2,288,128]{2,1,0:T(8,128)(2,1)S(1)} %join.1.refs_10_), channel_id=1, source_target_pairs={{0,2},{2,4},{4,6},{6,0},{1,3},{3,5},{5,7},{7,1},{8,10},{10,12},{12... | collective-permute-start | bytes 442376 | tf_op jit(solution)/shard_map/ppermute | solution.py:27
  108.8 11.1 %collective-permute-start.15 = (bf16[4,288,128]{2,1,0:T(8,128)(2,1)}, bf16[4,288,128]{2,1,0:T(8,128)(2,1)}, u32[]{:S(2)}, u32[]{:S(2)}) collective-permute-start(bf16[4,288,128]{2,1,0:T(8,128)(2,1)} %copy-done.7), channel_id=1, source_target_pairs={{0,1},{1,0},{2,3},{3,2},{4,5},{5,4},{6,7},{7,6},{8,9},{9,8},{10,11... | collective-permute-start | bytes 884744 | tf_op jit(solution)/shard_map/ppermute | solution.py:27
  114.4 4.4 %collective-permute-start.22 = (bf16[2,288,128]{2,1,0:T(8,128)(2,1)S(1)}, bf16[2,288,128]{2,1,0:T(8,128)(2,1)}, u32[]{:S(2)}, u32[]{:S(2)}) collective-permute-start(bf16[2,288,128]{2,1,0:T(8,128)(2,1)S(1)} %collective-permute-done.18.refs_13_), channel_id=1, source_target_pairs={{0,1},{1,0},{2,3},{3,2},{4,5},{5,4},{6,7},{7,6},{8,9},{9,8},{10,11... | collective-permute-start | bytes 442376 | tf_op jit(solution)/shard_map/ppermute | solution.py:27
  115.7 3.2 %collective-permute-start.21 = (bf16[2,288,128]{2,1,0:T(8,128)(2,1)S(1)}, bf16[2,288,128]{2,1,0:T(8,128)(2,1)}, u32[]{:S(2)}, u32[]{:S(2)}) collective-permute-start(bf16[2,288,128]{2,1,0:T(8,128)(2,1)S(1)} %collective-permute-done.17.refs_12_), channel_id=1, source_target_pairs={{0,1},{1,0},{2,3},{3,2},{4,5},{5,4},{6,7},{7,6},{8,9},{9,8},{10,11... | collective-permute-start | bytes 442376 | tf_op jit(solution)/shard_map/ppermute | solution.py:27
  118.0 1.7 collective-permute-start.20
  118.0 34.3 %copy-start.2 = (bf16[144,1152]{1,0:T(8,128)(2,1)S(1)}, bf16[144,1152]{1,0:T(8,128)(2,1)}, u32[]{:S(2)}) copy-start(bf16[144,1152]{1,0:T(8,128)(2,1)} %copy-done.1) | copy-start | bytes 995332
  118.0 34.3 %copy-start.4 = (bf16[144,1152]{1,0:T(8,128)(2,1)S(1)}, bf16[144,1152]{1,0:T(8,128)(2,1)}, u32[]{:S(2)}) copy-start(bf16[144,1152]{1,0:T(8,128)(2,1)} %copy-done.3) | copy-start | bytes 995332
  118.0 34.3 %copy-start.6 = (bf16[144,1152]{1,0:T(8,128)(2,1)S(1)}, bf16[144,1152]{1,0:T(8,128)(2,1)}, u32[]{:S(2)}) copy-start(bf16[144,1152]{1,0:T(8,128)(2,1)} %copy-done.5) | copy-start | bytes 995332
  118.0 34.3 %copy-start.8 = (bf16[4,288,128]{2,1,0:T(8,128)(2,1)S(1)}, bf16[4,288,128]{2,1,0:T(8,128)(2,1)}, u32[]{:S(2)}) copy-start(bf16[4,288,128]{2,1,0:T(8,128)(2,1)} %copy-done.7) | copy-start | bytes 884740
  118.0 34.3 %copy-start.9 = (f32[3,2240]{1,0:T(4,128)S(1)}, f32[3,2240]{1,0:T(4,128)}, u32[]{:S(2)}) copy-start(f32[3,2240]{1,0:T(4,128)} %refs_42_.1) | copy-start | bytes 80644
  118.0 22.1 %collective-permute-start.39 = (bf16[2,144,1152]{2,1,0:T(8,128)(2,1)S(1)}, bf16[2,144,1152]{2,1,0:T(8,128)(2,1)S(1)}, u32[]{:S(2)}, u32[]{:S(2)}) collective-permute-start(bf16[2,144,1152]{2,1,0:T(8,128)(2,1)S(1)} %pack.1.refs_21_), channel_id=1, source_target_pairs={{0,1},{1,0},{2,3},{3,2},{4,5},{5,4},{6,7},{7,6},{8,9},{9,8},{10,11... | collective-permute-start | bytes 1990664 | tf_op jit(solution)/shard_map/ppermute | solution.py:27
  118.8 4.2 %collective-permute-start.40 = (bf16[144,1152]{1,0:T(8,128)(2,1)}, bf16[144,1152]{1,0:T(8,128)(2,1)S(1)}, u32[]{:S(2)}, u32[]{:S(2)}) collective-permute-start(bf16[144,1152]{1,0:T(8,128)(2,1)} %copy-done.3), channel_id=1, source_target_pairs={{0,1},{1,0},{2,3},{3,2},{4,5},{5,4},{6,7},{7,6},{8,9},{9,8},{10,11... | collective-permute-start | bytes 995336 | tf_op jit(solution)/shard_map/ppermute | solution.py:27
  118.9 3.8 %collective-permute-start.14 = (bf16[4,288,128]{2,1,0:T(8,128)(2,1)}, bf16[4,288,128]{2,1,0:T(8,128)(2,1)S(1)}, u32[]{:S(2)}, u32[]{:S(2)}) collective-permute-start(bf16[4,288,128]{2,1,0:T(8,128)(2,1)} %collective-permute-done.10.refs_4_), channel_id=1, source_target_pairs={{0,1},{1,0},{2,3},{3,2},{4,5},{5,4},{6,7},{7,6},{8,9},{9,8},{10,11... | collective-permute-start | bytes 884744 | tf_op jit(solution)/shard_map/ppermute | solution.py:27
  119.7 3.2 %collective-permute-start.13 = (bf16[4,288,128]{2,1,0:T(8,128)(2,1)}, bf16[4,288,128]{2,1,0:T(8,128)(2,1)S(1)}, u32[]{:S(2)}, u32[]{:S(2)}) collective-permute-start(bf16[4,288,128]{2,1,0:T(8,128)(2,1)} %collective-permute-done.9.refs_3_), channel_id=1, source_target_pairs={{0,1},{1,0},{2,3},{3,2},{4,5},{5,4},{6,7},{7,6},{8,9},{9,8},{10,11... | collective-permute-start | bytes 884744 | tf_op jit(solution)/shard_map/ppermute | solution.py:27
  119.8 17.2 %collective-permute-start.34 = (bf16[2,144,1152]{2,1,0:T(8,128)(2,1)S(1)}, bf16[2,144,1152]{2,1,0:T(8,128)(2,1)S(1)}, u32[]{:S(2)}, u32[]{:S(2)}) collective-permute-start(bf16[2,144,1152]{2,1,0:T(8,128)(2,1)S(1)} %collective-permute-done.29.refs_23_), channel_id=1, source_target_pairs={{0,64},{64,128},{128,192},{192,0},{1,65},{65,129},{129,193},{193,1... | collective-permute-start | bytes 1990664 | tf_op jit(solution)/shard_map/ppermute | solution.py:27
  122.7 28.5 %collective-permute-start.5 = (bf16[2,2240,128]{2,1,0:T(8,128)(2,1)S(1)}, bf16[2,2240,128]{2,1,0:T(8,128)(2,1)S(1)}, u32[]{:S(2)}, u32[]{:S(2)}) collective-permute-start(bf16[2,2240,128]{2,1,0:T(8,128)(2,1)S(1)} %broadcast_select_fusion), channel_id=1, source_target_pairs={{0,8},{8,16},{16,24},{24,32},{32,40},{40,48},{48,56},{56,0},{1,9},... | collective-permute-start | bytes 3440648 | tf_op jit(solution)/shard_map/ppermute | solution.py:27
  122.8 17.2 %collective-permute-start.45 = (bf16[144,1152]{1,0:T(8,128)(2,1)}, bf16[144,1152]{1,0:T(8,128)(2,1)S(1)}, u32[]{:S(2)}, u32[]{:S(2)}) collective-permute-start(bf16[144,1152]{1,0:T(8,128)(2,1)} %collective-permute-done.33.refs_27_), channel_id=1, source_target_pairs={{0,1},{1,0},{2,3},{3,2},{4,5},{5,4},{6,7},{7,6},{8,9},{9,8},{10,11... | collective-permute-start | bytes 995336 | tf_op jit(solution)/shard_map/ppermute | solution.py:27
  123.0 17.6 %collective-permute-start.44 = (bf16[144,1152]{1,0:T(8,128)(2,1)}, bf16[144,1152]{1,0:T(8,128)(2,1)S(1)}, u32[]{:S(2)}, u32[]{:S(2)}) collective-permute-start(bf16[144,1152]{1,0:T(8,128)(2,1)} %collective-permute-done.32.refs_26_), channel_id=1, source_target_pairs={{0,1},{1,0},{2,3},{3,2},{4,5},{5,4},{6,7},{7,6},{8,9},{9,8},{10,11... | collective-permute-start | bytes 995336 | tf_op jit(solution)/shard_map/ppermute | solution.py:27
  137.0 10.4 %collective-permute-start.35 = (bf16[144,1152]{1,0:T(8,128)(2,1)}, bf16[144,1152]{1,0:T(8,128)(2,1)S(1)}, u32[]{:S(2)}, u32[]{:S(2)}) collective-permute-start(bf16[144,1152]{1,0:T(8,128)(2,1)} %collective-permute-done.32.refs_26_), channel_id=1, source_target_pairs={{0,192},{64,0},{128,64},{192,128},{1,193},{65,1},{129,65},{193,129... | collective-permute-start | bytes 995336 | tf_op jit(solution)/shard_map/ppermute | solution.py:27
  140.1 7.3 %collective-permute-start.43 = (bf16[144,1152]{1,0:T(8,128)(2,1)}, bf16[144,1152]{1,0:T(8,128)(2,1)S(1)}, u32[]{:S(2)}, u32[]{:S(2)}) collective-permute-start(bf16[144,1152]{1,0:T(8,128)(2,1)} %collective-permute-done.31.refs_25_), channel_id=1, source_target_pairs={{0,1},{1,0},{2,3},{3,2},{4,5},{5,4},{6,7},{7,6},{8,9},{9,8},{10,11... | collective-permute-start | bytes 995336 | tf_op jit(solution)/shard_map/ppermute | solution.py:27
  140.1 9.9 %collective-permute-start.42 = (bf16[2,144,1152]{2,1,0:T(8,128)(2,1)S(1)}, bf16[2,144,1152]{2,1,0:T(8,128)(2,1)S(1)}, u32[]{:S(2)}, u32[]{:S(2)}) collective-permute-start(bf16[2,144,1152]{2,1,0:T(8,128)(2,1)S(1)} %collective-permute-done.30.refs_24_), channel_id=1, source_target_pairs={{0,1},{1,0},{2,3},{3,2},{4,5},{5,4},{6,7},{7,6},{8,9},{9,8},{10,11... | collective-permute-start | bytes 1990664 | tf_op jit(solution)/shard_map/ppermute | solution.py:27
  140.6 9.4 %collective-permute-start.41 = (bf16[2,144,1152]{2,1,0:T(8,128)(2,1)S(1)}, bf16[2,144,1152]{2,1,0:T(8,128)(2,1)S(1)}, u32[]{:S(2)}, u32[]{:S(2)}) collective-permute-start(bf16[2,144,1152]{2,1,0:T(8,128)(2,1)S(1)} %collective-permute-done.29.refs_23_), channel_id=1, source_target_pairs={{0,1},{1,0},{2,3},{3,2},{4,5},{5,4},{6,7},{7,6},{8,9},{9,8},{10,11... | collective-permute-start | bytes 1990664 | tf_op jit(solution)/shard_map/ppermute | solution.py:27
  147.4 3.9 %collective-permute-start.46 = (bf16[2,144,1152]{2,1,0:T(8,128)(2,1)S(1)}, bf16[2,144,1152]{2,1,0:T(8,128)(2,1)S(1)}, u32[]{:S(2)}, u32[]{:S(2)}) collective-permute-start(bf16[2,144,1152]{2,1,0:T(8,128)(2,1)S(1)} %collective-permute-done.34.refs_28_), channel_id=1, source_target_pairs={{0,1},{1,0},{2,3},{3,2},{4,5},{5,4},{6,7},{7,6},{8,9},{9,8},{10,11... | collective-permute-start | bytes 1990664 | tf_op jit(solution)/shard_map/ppermute | solution.py:27
  147.4 2.6 %collective-permute-start.47 = (bf16[144,1152]{1,0:T(8,128)(2,1)S(1)}, bf16[144,1152]{1,0:T(8,128)(2,1)S(1)}, u32[]{:S(2)}, u32[]{:S(2)}) collective-permute-start(bf16[144,1152]{1,0:T(8,128)(2,1)S(1)} %collective-permute-done.35.refs_29_), channel_id=1, source_target_pairs={{0,1},{1,0},{2,3},{3,2},{4,5},{5,4},{6,7},{7,6},{8,9},{9,8},{10,11... | collective-permute-start | bytes 995336 | tf_op jit(solution)/shard_map/ppermute | solution.py:27
  151.3 1.0 copy-start.11

commit v2 on v1

--- a/solution.py
+++ b/solution.py
@@ -42,22 +42,17 @@
     tokens = k_ref.shape[2]
     pad = jnp.zeros((LANES - HEAD_DIM, tokens), jnp.bfloat16)
     ones = (lax.broadcasted_iota(jnp.int32, (LANES, tokens), 0) == HEAD_DIM).astype(jnp.bfloat16)
-
-    @pl.loop(0, 2)
-    def _(half):
-        for inner in range(HALF_HEADS):
-            start = half * (HALF_HEADS * HEAD_DIM) + inner * HEAD_DIM
-            rows = pl.ds(pl.multiple_of(start, 16), HEAD_DIM)
-            keys = jnp.maximum(k_ref[0, rows, :], 0)
-            vals = v_ref[0, rows, :]
-            left = jnp.concatenate([vals, keys], axis=1)
-            right = jnp.concatenate([jnp.concatenate([keys, pad], axis=0), ones], axis=1)
-            part = lax.dot_general(
-                left, right, (((1,), (1,)), ((), ())), preferred_element_type=jnp.float32
-            )
-            rows = slice(inner * HEAD_DIM, (inner + 1) * HEAD_DIM)
-            acc_ref[half, rows, :] = acc_ref[half, rows, :] + part
-
+    for head in range(HEADS):
+        half, inner = divmod(head, HALF_HEADS)
+        keys = jnp.maximum(k_ref[0, head * HEAD_DIM : (head + 1) * HEAD_DIM, :], 0)
+        vals = v_ref[0, head * HEAD_DIM : (head + 1) * HEAD_DIM, :]
+        left = jnp.concatenate([vals, keys], axis=1)
+        right = jnp.concatenate([jnp.concatenate([keys, pad], axis=0), ones], axis=1)
+        part = lax.dot_general(
+            left, right, (((1,), (1,)), ((), ())), preferred_element_type=jnp.float32
+        )
+        rows = slice(inner * HEAD_DIM, (inner + 1) * HEAD_DIM)
+        acc_ref[half, rows, :] = acc_ref[half, rows, :] + part
     norm = lax.broadcasted_iota(jnp.int32, (PADDED, LANES), 1) == HEAD_DIM
     for ref, half in ((mine_ref, core), (theirs_ref, 1 - core)):
         for pair in range(HALF_ROWS // PAIR):
@@ -323,34 +318,29 @@
     def _():
         pad = jnp.zeros((LANES - HEAD_DIM, tokens), jnp.bfloat16)
         lanes = pl.ds(pl.multiple_of(step * tokens, tokens), tokens)
-
-        @pl.loop(0, 2)
-        def _(half):
-            for inner in range(HALF_HEADS):
-                start = half * (HALF_HEADS * HEAD_DIM) + inner * HEAD_DIM
-                query = query_ref[pl.ds(pl.multiple_of(start, 16), HEAD_DIM), :]
-                first = padded_row(inner * HEAD_DIM)
-                low = first // 16 * 16
-                high = -(-(padded_row(inner * HEAD_DIM + HEAD_DIM - 1) + 1) // 16) * 16
-                top = jnp.dot(
-                    state_ref[half, low:high, :],
-                    jnp.concatenate([query, pad], axis=0),
-                    preferred_element_type=jnp.float32,
-                )
-                norm = state_ref[half, inner * HEAD_DIM : (inner + 1) * HEAD_DIM, HEAD_DIM : HEAD_DIM + 1]
-                bottom = norm.astype(jnp.float32) * query.astype(jnp.float32)
-                bottom = jnp.sum(bottom, axis=0, keepdims=True) + stab_eps
-                result = top * (1.0 / bottom)
-                base = pl.multiple_of(half * HALF_ROWS + low, 16)
-                if first > low:
-                    edge = pl.ds(base, 16)
-                    held = att_ref[edge, lanes].astype(jnp.float32)
-                    keep = lax.broadcasted_iota(jnp.int32, (16, tokens), 0) < first - low
-                    att_ref[edge, lanes] = jnp.where(keep, held, result[:16]).astype(att_ref.dtype)
-                    inside = pl.ds(pl.multiple_of(base + 16, 16), high - low - 16)
-                    att_ref[inside, lanes] = result[16:].astype(att_ref.dtype)
-                else:
-                    att_ref[pl.ds(base, high - low), lanes] = result.astype(att_ref.dtype)
+        for head in range(HEADS):
+            half, inner = divmod(head, HALF_HEADS)
+            query = query_ref[head * HEAD_DIM : (head + 1) * HEAD_DIM, :]
+            first = padded_row(inner * HEAD_DIM)
+            low = first // 16 * 16
+            high = -(-(padded_row(inner * HEAD_DIM + HEAD_DIM - 1) + 1) // 16) * 16
+            top = jnp.dot(
+                state_ref[half, low:high, :],
+                jnp.concatenate([query, pad], axis=0),
+                preferred_element_type=jnp.float32,
+            )
+            norm = state_ref[half, inner * HEAD_DIM : (inner + 1) * HEAD_DIM, HEAD_DIM : HEAD_DIM + 1]
+            bottom = norm.astype(jnp.float32) * query.astype(jnp.float32)
+            bottom = jnp.sum(bottom, axis=0, keepdims=True) + stab_eps
+            result = top * (1.0 / bottom)
+            base = half * HALF_ROWS
+            if first > low:
+                held = att_ref[base + low : base + low + 16, lanes].astype(jnp.float32)
+                keep = lax.broadcasted_iota(jnp.int32, (16, tokens), 0) < first - low
+                att_ref[base + low : base + low + 16, lanes] = jnp.where(keep, held, result[:16]).astype(att_ref.dtype)
+                att_ref[base + low + 16 : base + high, lanes] = result[16:].astype(att_ref.dtype)
+            else:
+                att_ref[base + low : base + high, lanes] = result.astype(att_ref.dtype)
 
     @pl.when(step == steps)
     def _():

time: 177 us -> 176 us (level)
  no operation moved by 1% of the time
where the time goes in v2:
time: 176 us; the launch traced here: 174 us
  waiting for transfers between devices  76.3 us (43%)
  starting transfers between devices  59.7 us (34%)
  Pallas kernels  31.7 us (18%)
  local copies, waits for them, and re-layouts  4.27 us (2%)
    ppermute x46, waiting for transfers between devices, shift(): lax.ppermute(value, axis, [(i, (i + distance) % size) for i in range(size)])  60.5 us
    ppermute x46, starting transfers between devices, shift(): lax.ppermute(value, axis, [(i, (i + distance) % size) for i in range(size)])  42.3 us
    pallas_call x1, Pallas kernels, tail(): pl.pallas_call(functools.partial(tail_kernel, spots), out_shape=jax.Shape...  22 us
    all_to_all x1, waiting for transfers between devices, layer(): before = lax.all_to_all(cuts, ('x', 'z'), 0, 0)  8.9 us
    all_to_all x1, starting transfers between devices, layer(): before = lax.all_to_all(cuts, ('x', 'z'), 0, 0)  7.77 us
    all_to_all x1, starting transfers between devices, layer(): cuts = lax.all_to_all(cuts, ('x', 'z'), 0, 0)  5.9 us
    pallas_call x1, Pallas kernels, local_kv(): pl.pallas_call(kv_kernel, out_shape=[jax.ShapeDtypeStruct((frames, HALF_R...  5.47 us
    ppermute x1, waiting for transfers between devices, layer(): partner = lax.ppermute(block, 'z', [(i, i ^ 1) for i in range(nz)])  4.81 us
  transfers between devices with their start and end apart: 50, of which 21 were waited for; matrix products, arithmetic and copies ran while one was open for 2% of the time, Pallas kernels for 2%

profile of v2, /device:TPU:2, one launch (start us, length us, event | category | flops | bytes accessed | tf_op | source)
XLA Modules:
  0.0 173.9 jit_solution(16674644190983227871)
XLA Ops:
  0.0 5.5 %local_kv.1 = (bf16[4,1152,128]{2,1,0:T(8,128)(2,1)}, bf16[4,1152,128]{2,1,0:T(8,128)(2,1)}) custom-call(s32[1]{0:T(128)} %bitcast.core_ref, bf16[4,2240,128]{2,1,0:T(8,128)(2,1)} %bitcast.8, bf16[4,2240,128]{2,1,0:T(8,128)(2,1)} %bitcast.9), custom_call_target="tpu_custom_call" | custom-call | flops 587202560 | bytes 9175040 | tf_op jit(solution)/shard_map/local_kv/pallas_call | solution.py:74
  5.5 2.4 %slice.4 = bf16[2,2240,128]{2,1,0:T(8,128)(2,1)} slice(bf16[4,2240,128]{2,1,0:T(8,128)(2,1)} %bitcast.10), slice={[2:4], [0:2240], [0:128]} | slice | bytes 2293760 | tf_op jit(solution)/shard_map/slice | solution.py:421
  7.9 1.7 collective-permute-start
  9.7 2.0 %collective-permute-start.23 = (bf16[72,1152]{1,0:T(8,128)(2,1)S(1)}, bf16[72,1152]{1,0:T(8,128)(2,1)S(1)}, u32[]{:S(2)}, u32[]{:S(2)}) collective-permute-start(bf16[72,1152]{1,0:T(8,128)(2,1)S(1)} %pad_dynamic-slice_fusion.mine_ref), channel_id=1, source_target_pairs={{0,8},{8,0},{16,24},{24,16},{32,40},{40,32},{48,56},{56,48},{1,9},... | collective-permute-start | bytes 497672 | tf_op jit(solution)/shard_map/ppermute | solution.py:420
  11.7 4.8 %collective-permute-done.23.other_ref = bf16[72,1152]{1,0:T(8,128)(2,1)S(1)} collective-permute-done((bf16[72,1152]{1,0:T(8,128)(2,1)S(1)}, bf16[72,1152]{1,0:T(8,128)(2,1)S(1)}, u32[]{:S(2)}, u32[]{:S(2)}) %collective-permute-start.23) | collective-permute-done | bytes 165920 | tf_op jit(solution)/shard_map/ppermute | solution.py:420
  16.5 0.6 in_order.1.refs_18_
  17.1 6.9 %collective-permute-start.26 = (bf16[144,1152]{1,0:T(8,128)(2,1)S(1)}, bf16[144,1152]{1,0:T(8,128)(2,1)}, u32[]{:S(2)}, u32[]{:S(2)}) collective-permute-start(bf16[144,1152]{1,0:T(8,128)(2,1)S(1)} %in_order.1.refs_18_), channel_id=1, source_target_pairs={{0,48},{8,56},{16,0},{24,8},{32,16},{40,24},{48,32},{56,40},{1,49}... | collective-permute-start | bytes 995336 | tf_op jit(solution)/shard_map/ppermute | solution.py:27
  24.1 0.8 split.1
  24.9 1.6 collective-permute-start.2
  26.5 2.9 %collective-permute-start.3 = (bf16[2,288,128]{2,1,0:T(8,128)(2,1)S(1)}, bf16[2,288,128]{2,1,0:T(8,128)(2,1)S(1)}, u32[]{:S(2)}, u32[]{:S(2)}) collective-permute-start(bf16[2,288,128]{2,1,0:T(8,128)(2,1)S(1)} %get-tuple-element.48), channel_id=1, source_target_pairs={{0,4},{2,6},{4,0},{6,2},{1,5},{3,7},{5,1},{7,3},{8,12},{10,14},{12... | collective-permute-start | bytes 442376 | tf_op jit(solution)/shard_map/ppermute | solution.py:27
  29.4 1.3 collective-permute-start.4
  30.7 1.0 collective-permute-done.2.a_ref
  31.7 3.9 %collective-permute-done.3.b_ref = bf16[2,288,128]{2,1,0:T(8,128)(2,1)S(1)} collective-permute-done((bf16[2,288,128]{2,1,0:T(8,128)(2,1)S(1)}, bf16[2,288,128]{2,1,0:T(8,128)(2,1)S(1)}, u32[]{:S(2)}, u32[]{:S(2)}) %collective-permute-start.3) | collective-permute-done | bytes 147488 | tf_op jit(solution)/shard_map/ppermute | solution.py:27
  35.6 0.8 total.1
  36.4 1.1 collective-permute-start.6
  37.5 2.7 %collective-permute-start.7 = (bf16[2,288,128]{2,1,0:T(8,128)(2,1)}, bf16[2,288,128]{2,1,0:T(8,128)(2,1)S(1)}, u32[]{:S(2)}, u32[]{:S(2)}) collective-permute-start(bf16[2,288,128]{2,1,0:T(8,128)(2,1)} %get-tuple-element.57), channel_id=1, source_target_pairs={{0,4},{2,6},{4,0},{6,2},{1,5},{3,7},{5,1},{7,3},{8,12},{10,14},{12... | collective-permute-start | bytes 442376 | tf_op jit(solution)/shard_map/ppermute | solution.py:27
  40.2 1.5 collective-permute-start.25
  41.7 2.6 %collective-permute-done.6.a_ref = bf16[2,288,128]{2,1,0:T(8,128)(2,1)S(1)} collective-permute-done((bf16[2,288,128]{2,1,0:T(8,128)(2,1)S(1)}, bf16[2,288,128]{2,1,0:T(8,128)(2,1)S(1)}, u32[]{:S(2)}, u32[]{:S(2)}) %collective-permute-start.6) | collective-permute-done | bytes 147488 | tf_op jit(solution)/shard_map/ppermute | solution.py:27
  44.3 1.2 collective-permute-start.24
  45.5 5.9 %all-to-all-start = ((bf16[32,18,128]{2,1,0:T(8,128)(2,1)}), bf16[32,18,128]{2,1,0:T(8,128)(2,1)S(1)}, u32[]{:S(2)}, u32[]{:S(2)}) async-start(bf16[32,18,128]{2,1,0:T(8,128)(2,1)} %get-tuple-element.50), calls=%async_computation | async-start | bytes 393216 | tf_op jit(solution)/shard_map/all_to_all | solution.py:434
  51.4 1.1 collective-permute-start.8
  52.5 4.2 %collective-permute-done.8.c_ref = bf16[2,288,128]{2,1,0:T(8,128)(2,1)S(1)} collective-permute-done((bf16[2,288,128]{2,1,0:T(8,128)(2,1)S(1)}, bf16[2,288,128]{2,1,0:T(8,128)(2,1)S(1)}, u32[]{:S(2)}, u32[]{:S(2)}) %collective-permute-start.8) | collective-permute-done | bytes 147488 | tf_op jit(solution)/shard_map/ppermute | solution.py:27
  56.7 3.6 %collective-permute-start.28 = (bf16[144,1152]{1,0:T(8,128)(2,1)}, bf16[144,1152]{1,0:T(8,128)(2,1)S(1)}, u32[]{:S(2)}, u32[]{:S(2)}) collective-permute-start(bf16[144,1152]{1,0:T(8,128)(2,1)} %collective-permute-done.26.refs_0_), channel_id=1, source_target_pairs={{0,48},{8,56},{16,0},{24,8},{32,16},{40,24},{48,32},{56,40},{1,49}... | collective-permute-start | bytes 995336 | tf_op jit(solution)/shard_map/ppermute | solution.py:27
  60.2 2.1 %all-to-all-done.in_ref = bf16[32,18,128]{2,1,0:T(8,128)(2,1)S(1)} async-done(((bf16[32,18,128]{2,1,0:T(8,128)(2,1)}), bf16[32,18,128]{2,1,0:T(8,128)(2,1)S(1)}, u32[]{:S(2)}, u32[]{:S(2)}) %all-to-all-start) | async-done | bytes 147488 | tf_op jit(solution)/shard_map/all_to_all | solution.py:434
  62.3 0.8 exclusive_scan.1
  63.2 0.6 collective-permute-start.11
  63.8 1.2 collective-permute-start.10
  64.9 0.5 collective-permute-start.9
  65.4 6.7 %collective-permute-done.28.refs_22_ = bf16[144,1152]{1,0:T(8,128)(2,1)S(1)} collective-permute-done((bf16[144,1152]{1,0:T(8,128)(2,1)}, bf16[144,1152]{1,0:T(8,128)(2,1)S(1)}, u32[]{:S(2)}, u32[]{:S(2)}) %collective-permute-start.28) | collective-permute-done | bytes 331808 | tf_op jit(solution)/shard_map/ppermute | solution.py:27
  72.1 0.6 collective-permute-start.33
  72.7 0.5 collective-permute-done.11.refs_5_
  73.2 1.1 pack.1.refs_21_
  74.3 1.0 collective-permute-done.10.refs_4_
  75.3 1.8 %collective-permute-start.30 = (bf16[2,144,1152]{2,1,0:T(8,128)(2,1)S(1)}, bf16[2,144,1152]{2,1,0:T(8,128)(2,1)S(1)}, u32[]{:S(2)}, u32[]{:S(2)}) collective-permute-start(bf16[2,144,1152]{2,1,0:T(8,128)(2,1)S(1)} %pack.1.refs_21_), channel_id=1, source_target_pairs={{0,192},{64,0},{128,64},{192,128},{1,193},{65,1},{129,65},{193,129... | collective-permute-start | bytes 1990664 | tf_op jit(solution)/shard_map/ppermute | solution.py:27
  77.1 2.3 %collective-permute-done.9.refs_3_ = bf16[4,288,128]{2,1,0:T(8,128)(2,1)} collective-permute-done((bf16[4,288,128]{2,1,0:T(8,128)(2,1)S(1)}, bf16[4,288,128]{2,1,0:T(8,128)(2,1)}, u32[]{:S(2)}, u32[]{:S(2)}) %collective-permute-start.9) | collective-permute-done | bytes 294944 | tf_op jit(solution)/shard_map/ppermute | solution.py:27
  79.4 1.4 collective-permute-start.29
  80.8 0.7 copy-done.5
  81.5 7.8 %all-to-all-start.1 = ((bf16[32,18,128]{2,1,0:T(8,128)(2,1)}), bf16[32,18,128]{2,1,0:T(8,128)(2,1)S(1)}, u32[]{:S(2)}, u32[]{:S(2)}) async-start(bf16[32,18,128]{2,1,0:T(8,128)(2,1)} %exclusive_scan.1), calls=%async_computation.1 | async-start | bytes 393216 | tf_op jit(solution)/shard_map/all_to_all | solution.py:442
  89.3 0.3 collective-permute-start.32
  89.6 1.8 %collective-permute-start.31 = (bf16[144,1152]{1,0:T(8,128)(2,1)}, bf16[144,1152]{1,0:T(8,128)(2,1)}, u32[]{:S(2)}, u32[]{:S(2)}) collective-permute-start(bf16[144,1152]{1,0:T(8,128)(2,1)} %copy-done.3), channel_id=1, source_target_pairs={{0,64},{64,128},{128,192},{192,0},{1,65},{65,129},{129,193},{193,1... | collective-permute-start | bytes 995336 | tf_op jit(solution)/shard_map/ppermute | solution.py:27
  91.4 8.9 %all-to-all-done.1.in_ref = bf16[32,18,128]{2,1,0:T(8,128)(2,1)S(1)} async-done(((bf16[32,18,128]{2,1,0:T(8,128)(2,1)}), bf16[32,18,128]{2,1,0:T(8,128)(2,1)S(1)}, u32[]{:S(2)}, u32[]{:S(2)}) %all-to-all-start.1) | async-done | bytes 147488 | tf_op jit(solution)/shard_map/all_to_all | solution.py:442
  100.5 4.3 %collective-permute-done.32.refs_26_ = bf16[144,1152]{1,0:T(8,128)(2,1)} collective-permute-done((bf16[144,1152]{1,0:T(8,128)(2,1)}, bf16[144,1152]{1,0:T(8,128)(2,1)}, u32[]{:S(2)}, u32[]{:S(2)}) %collective-permute-start.32) | collective-permute-done | bytes 331808 | tf_op jit(solution)/shard_map/ppermute | solution.py:27
  104.8 0.7 collective-permute-done.31.refs_25_
  105.5 1.3 collective-permute-start.18
  106.8 1.3 collective-permute-start.16
  108.1 5.7 %collective-permute-done.18.refs_13_ = bf16[2,288,128]{2,1,0:T(8,128)(2,1)S(1)} collective-permute-done((bf16[2,288,128]{2,1,0:T(8,128)(2,1)S(1)}, bf16[2,288,128]{2,1,0:T(8,128)(2,1)S(1)}, u32[]{:S(2)}, u32[]{:S(2)}) %collective-permute-start.18) | collective-permute-done | bytes 147488 | tf_op jit(solution)/shard_map/ppermute | solution.py:27
  113.8 1.3 collective-permute-done.17.refs_12_
  115.1 2.3 %collective-permute-done.16.refs_11_ = bf16[2,288,128]{2,1,0:T(8,128)(2,1)} collective-permute-done((bf16[2,288,128]{2,1,0:T(8,128)(2,1)S(1)}, bf16[2,288,128]{2,1,0:T(8,128)(2,1)}, u32[]{:S(2)}, u32[]{:S(2)}) %collective-permute-start.16) | collective-permute-done | bytes 147488 | tf_op jit(solution)/shard_map/ppermute | solution.py:27
  117.4 0.6 collective-permute-start.39
  118.1 0.4 collective-permute-start.14
  118.5 0.6 collective-permute-done.20.refs_15_
  119.2 1.5 collective-permute-start.34
  120.7 1.4 broadcast_select_fusion
  122.2 0.2 collective-permute-start.45
  122.4 0.4 collective-permute-start.44
  122.8 13.6 %collective-permute-done.34.refs_28_ = bf16[2,144,1152]{2,1,0:T(8,128)(2,1)S(1)} collective-permute-done((bf16[2,144,1152]{2,1,0:T(8,128)(2,1)S(1)}, bf16[2,144,1152]{2,1,0:T(8,128)(2,1)S(1)}, u32[]{:S(2)}, u32[]{:S(2)}) %collective-permute-start.34) | collective-permute-done | bytes 663584 | tf_op jit(solution)/shard_map/ppermute | solution.py:27
  136.4 3.1 %collective-permute-start.35 = (bf16[144,1152]{1,0:T(8,128)(2,1)}, bf16[144,1152]{1,0:T(8,128)(2,1)S(1)}, u32[]{:S(2)}, u32[]{:S(2)}) collective-permute-start(bf16[144,1152]{1,0:T(8,128)(2,1)} %collective-permute-done.32.refs_26_), channel_id=1, source_target_pairs={{0,192},{64,0},{128,64},{192,128},{1,193},{65,1},{129,65},{193,129... | collective-permute-start | bytes 995336 | tf_op jit(solution)/shard_map/ppermute | solution.py:27
  139.5 0.5 collective-permute-start.42
  140.1 6.7 %collective-permute-done.35.refs_29_ = bf16[144,1152]{1,0:T(8,128)(2,1)S(1)} collective-permute-done((bf16[144,1152]{1,0:T(8,128)(2,1)}, bf16[144,1152]{1,0:T(8,128)(2,1)S(1)}, u32[]{:S(2)}, u32[]{:S(2)}) %collective-permute-start.35) | collective-permute-done | bytes 331808 | tf_op jit(solution)/shard_map/ppermute | solution.py:27
  146.8 0.5 collective-permute-start.47
  147.4 2.0 %collective-permute-done.47.refs_41_ = bf16[144,1152]{1,0:T(8,128)(2,1)S(1)} collective-permute-done((bf16[144,1152]{1,0:T(8,128)(2,1)S(1)}, bf16[144,1152]{1,0:T(8,128)(2,1)S(1)}, u32[]{:S(2)}, u32[]{:S(2)}) %collective-permute-start.47) | collective-permute-done | bytes 331808 | tf_op jit(solution)/shard_map/ppermute | solution.py:27
  149.4 1.3 collective-permute-done.5.refs_0_
  150.7 1.0 copy-done.11
  151.7 22.0 %tail.1 = bf16[4,2240,128]{2,1,0:T(8,128)(2,1)} custom-call(s32[4]{0:T(128)S(1)} %pad_add_fusion.where_ref, bf16[2,2240,128]{2,1,0:T(8,128)(2,1)} %copy-done.11, bf16[4,2240,128]{2,1,0:T(8,128)(2,1)} %bitcast.12, bf16[4,288,128]{2,1,0:T(8,128)(2,1)S(1)} %rest.1.refs_2_, bf16[4,288,128]{2,1,0:T(8,128)(2,1)} %collective-permute-done.9.refs_3_, ...), custom_call_target="tpu_custom_call" | custom-call | flops 8147435520 | bytes 10035200 | tf_op jit(solution)/shard_map/tail/pallas_call | solution.py:372
  (74 shorter events, 1.0 us)
Async XLA Ops:
  5.5 4.1 %copy-start.10 = (bf16[70,2240]{1,0:T(8,128)(2,1)S(1)}, bf16[70,2240]{1,0:T(8,128)(2,1)}, u32[]{:S(2)}) copy-start(bf16[70,2240]{1,0:T(8,128)(2,1)} %param.8) | copy-start | bytes 940804
  5.5 18.6 %collective-permute-start.1 = (bf16[4,1152,128]{2,1,0:T(8,128)(2,1)}, bf16[4,1152,128]{2,1,0:T(8,128)(2,1)S(1)}, u32[]{:S(2)}, u32[]{:S(2)}) collective-permute-start(bf16[4,1152,128]{2,1,0:T(8,128)(2,1)} %get-tuple-element.45), channel_id=1, source_target_pairs={{0,1},{1,0},{2,3},{3,2},{4,5},{5,4},{6,7},{7,6},{8,9},{9,8},{10,11... | collective-permute-start | bytes 3538952 | tf_op jit(solution)/shard_map/ppermute | solution.py:27
  5.5 18.6 %copy-start = (bf16[4,1152,128]{2,1,0:T(8,128)(2,1)S(1)}, bf16[4,1152,128]{2,1,0:T(8,128)(2,1)}, u32[]{:S(2)}) copy-start(bf16[4,1152,128]{2,1,0:T(8,128)(2,1)} %get-tuple-element.44.mine_ref) | copy-start | bytes 3538948
  7.9 57.5 %collective-permute-start = (bf16[2,2240,128]{2,1,0:T(8,128)(2,1)}, bf16[2,2240,128]{2,1,0:T(8,128)(2,1)}, u32[]{:S(2)}, u32[]{:S(2)}) collective-permute-start(bf16[2,2240,128]{2,1,0:T(8,128)(2,1)} %slice.4), channel_id=1, source_target_pairs={{56,120},{120,184},{184,248},{57,121},{121,185},{185,249},{58,122}... | collective-permute-start | bytes 3440648 | tf_op jit(solution)/shard_map/ppermute | solution.py:422
  9.7 6.9 %collective-permute-start.23 = (bf16[72,1152]{1,0:T(8,128)(2,1)S(1)}, bf16[72,1152]{1,0:T(8,128)(2,1)S(1)}, u32[]{:S(2)}, u32[]{:S(2)}) collective-permute-start(bf16[72,1152]{1,0:T(8,128)(2,1)S(1)} %pad_dynamic-slice_fusion.mine_ref), channel_id=1, source_target_pairs={{0,8},{8,0},{16,24},{24,16},{32,40},{40,32},{48,56},{56,48},{1,9},... | collective-permute-start | bytes 497672 | tf_op jit(solution)/shard_map/ppermute | solution.py:420
  17.1 23.1 %collective-permute-start.26 = (bf16[144,1152]{1,0:T(8,128)(2,1)S(1)}, bf16[144,1152]{1,0:T(8,128)(2,1)}, u32[]{:S(2)}, u32[]{:S(2)}) collective-permute-start(bf16[144,1152]{1,0:T(8,128)(2,1)S(1)} %in_order.1.refs_18_), channel_id=1, source_target_pairs={{0,48},{8,56},{16,0},{24,8},{32,16},{40,24},{48,32},{56,40},{1,49}... | collective-permute-start | bytes 995336 | tf_op jit(solution)/shard_map/ppermute | solution.py:27
  24.9 6.8 %collective-permute-start.2 = (bf16[2,288,128]{2,1,0:T(8,128)(2,1)S(1)}, bf16[2,288,128]{2,1,0:T(8,128)(2,1)S(1)}, u32[]{:S(2)}, u32[]{:S(2)}) collective-permute-start(bf16[2,288,128]{2,1,0:T(8,128)(2,1)S(1)} %get-tuple-element.47), channel_id=1, source_target_pairs={{0,2},{2,4},{4,6},{6,0},{1,3},{3,5},{5,7},{7,1},{8,10},{10,12},{12... | collective-permute-start | bytes 442376 | tf_op jit(solution)/shard_map/ppermute | solution.py:27
  26.5 9.1 %collective-permute-start.3 = (bf16[2,288,128]{2,1,0:T(8,128)(2,1)S(1)}, bf16[2,288,128]{2,1,0:T(8,128)(2,1)S(1)}, u32[]{:S(2)}, u32[]{:S(2)}) collective-permute-start(bf16[2,288,128]{2,1,0:T(8,128)(2,1)S(1)} %get-tuple-element.48), channel_id=1, source_target_pairs={{0,4},{2,6},{4,0},{6,2},{1,5},{3,7},{5,1},{7,3},{8,12},{10,14},{12... | collective-permute-start | bytes 442376 | tf_op jit(solution)/shard_map/ppermute | solution.py:27
  29.4 6.2 %collective-permute-start.4 = (bf16[2,288,128]{2,1,0:T(8,128)(2,1)S(1)}, bf16[2,288,128]{2,1,0:T(8,128)(2,1)S(1)}, u32[]{:S(2)}, u32[]{:S(2)}) collective-permute-start(bf16[2,288,128]{2,1,0:T(8,128)(2,1)S(1)} %get-tuple-element.49), channel_id=1, source_target_pairs={{0,6},{2,0},{4,2},{6,4},{1,7},{3,1},{5,3},{7,5},{8,14},{10,8},{12,... | collective-permute-start | bytes 442376 | tf_op jit(solution)/shard_map/ppermute | solution.py:27
  36.4 7.9 %collective-permute-start.6 = (bf16[2,288,128]{2,1,0:T(8,128)(2,1)S(1)}, bf16[2,288,128]{2,1,0:T(8,128)(2,1)S(1)}, u32[]{:S(2)}, u32[]{:S(2)}) collective-permute-start(bf16[2,288,128]{2,1,0:T(8,128)(2,1)S(1)} %get-tuple-element.54), channel_id=1, source_target_pairs={{0,2},{2,4},{4,6},{6,0},{1,3},{3,5},{5,7},{7,1},{8,10},{10,12},{12... | collective-permute-start | bytes 442376 | tf_op jit(solution)/shard_map/ppermute | solution.py:27
  37.5 13.9 %collective-permute-start.7 = (bf16[2,288,128]{2,1,0:T(8,128)(2,1)}, bf16[2,288,128]{2,1,0:T(8,128)(2,1)S(1)}, u32[]{:S(2)}, u32[]{:S(2)}) collective-permute-start(bf16[2,288,128]{2,1,0:T(8,128)(2,1)} %get-tuple-element.57), channel_id=1, source_target_pairs={{0,4},{2,6},{4,0},{6,2},{1,5},{3,7},{5,1},{7,3},{8,12},{10,14},{12... | collective-permute-start | bytes 442376 | tf_op jit(solution)/shard_map/ppermute | solution.py:27
  40.2 23.0 %collective-permute-start.27 = (bf16[144,1152]{1,0:T(8,128)(2,1)S(1)}, bf16[144,1152]{1,0:T(8,128)(2,1)S(1)}, u32[]{:S(2)}, u32[]{:S(2)}) collective-permute-start(bf16[144,1152]{1,0:T(8,128)(2,1)S(1)} %in_order.1.refs_18_), channel_id=1, source_target_pairs={{0,16},{8,24},{16,32},{24,40},{32,48},{40,56},{48,0},{56,8},{1,17}... | collective-permute-start | bytes 995336 | tf_op jit(solution)/shard_map/ppermute | solution.py:27
  40.2 23.6 %collective-permute-start.25 = (bf16[144,1152]{1,0:T(8,128)(2,1)S(1)}, bf16[144,1152]{1,0:T(8,128)(2,1)}, u32[]{:S(2)}, u32[]{:S(2)}) collective-permute-start(bf16[144,1152]{1,0:T(8,128)(2,1)S(1)} %in_order.1.refs_18_), channel_id=1, source_target_pairs={{0,192},{64,0},{128,64},{192,128},{1,193},{65,1},{129,65},{193,129... | collective-permute-start | bytes 995336 | tf_op jit(solution)/shard_map/ppermute | solution.py:27
  44.3 20.6 %collective-permute-start.24 = (bf16[144,1152]{1,0:T(8,128)(2,1)S(1)}, bf16[144,1152]{1,0:T(8,128)(2,1)S(1)}, u32[]{:S(2)}, u32[]{:S(2)}) collective-permute-start(bf16[144,1152]{1,0:T(8,128)(2,1)S(1)} %in_order.1.refs_18_), channel_id=1, source_target_pairs={{0,64},{64,128},{128,192},{192,0},{1,65},{65,129},{129,193},{193,1... | collective-permute-start | bytes 995336 | tf_op jit(solution)/shard_map/ppermute | solution.py:27
  45.5 16.8 %all-to-all-start = ((bf16[32,18,128]{2,1,0:T(8,128)(2,1)}), bf16[32,18,128]{2,1,0:T(8,128)(2,1)S(1)}, u32[]{:S(2)}, u32[]{:S(2)}) async-start(bf16[32,18,128]{2,1,0:T(8,128)(2,1)} %get-tuple-element.50), calls=%async_computation | async-start | bytes 393216 | tf_op jit(solution)/shard_map/all_to_all | solution.py:434
  51.4 5.2 %collective-permute-start.8 = (bf16[2,288,128]{2,1,0:T(8,128)(2,1)S(1)}, bf16[2,288,128]{2,1,0:T(8,128)(2,1)S(1)}, u32[]{:S(2)}, u32[]{:S(2)}) collective-permute-start(bf16[2,288,128]{2,1,0:T(8,128)(2,1)S(1)} %get-tuple-element.60), channel_id=1, source_target_pairs={{0,6},{2,0},{4,2},{6,4},{1,7},{3,1},{5,3},{7,5},{8,14},{10,8},{12,... | collective-permute-start | bytes 442376 | tf_op jit(solution)/shard_map/ppermute | solution.py:27
  56.7 15.4 %collective-permute-start.28 = (bf16[144,1152]{1,0:T(8,128)(2,1)}, bf16[144,1152]{1,0:T(8,128)(2,1)S(1)}, u32[]{:S(2)}, u32[]{:S(2)}) collective-permute-start(bf16[144,1152]{1,0:T(8,128)(2,1)} %collective-permute-done.26.refs_0_), channel_id=1, source_target_pairs={{0,48},{8,56},{16,0},{24,8},{32,16},{40,24},{48,32},{56,40},{1,49}... | collective-permute-start | bytes 995336 | tf_op jit(solution)/shard_map/ppermute | solution.py:27
  63.2 10.0 %collective-permute-start.11 = (bf16[4,288,128]{2,1,0:T(8,128)(2,1)S(1)}, bf16[4,288,128]{2,1,0:T(8,128)(2,1)S(1)}, u32[]{:S(2)}, u32[]{:S(2)}) collective-permute-start(bf16[4,288,128]{2,1,0:T(8,128)(2,1)S(1)} %rest.1.refs_2_), channel_id=1, source_target_pairs={{0,6},{2,0},{4,2},{6,4},{1,7},{3,1},{5,3},{7,5},{8,14},{10,8},{12,... | collective-permute-start | bytes 884744 | tf_op jit(solution)/shard_map/ppermute | solution.py:27
  63.8 11.5 %collective-permute-start.10 = (bf16[4,288,128]{2,1,0:T(8,128)(2,1)S(1)}, bf16[4,288,128]{2,1,0:T(8,128)(2,1)}, u32[]{:S(2)}, u32[]{:S(2)}) collective-permute-start(bf16[4,288,128]{2,1,0:T(8,128)(2,1)S(1)} %rest.1.refs_2_), channel_id=1, source_target_pairs={{0,4},{2,6},{4,0},{6,2},{1,5},{3,7},{5,1},{7,3},{8,12},{10,14},{12... | collective-permute-start | bytes 884744 | tf_op jit(solution)/shard_map/ppermute | solution.py:27
  64.9 9.4 %copy-start.1 = (bf16[144,1152]{1,0:T(8,128)(2,1)}, bf16[144,1152]{1,0:T(8,128)(2,1)S(1)}, u32[]{:S(2)}) copy-start(bf16[144,1152]{1,0:T(8,128)(2,1)S(1)} %collective-permute-done.24.refs_19_) | copy-start | bytes 995332
  64.9 14.4 %collective-permute-start.9 = (bf16[4,288,128]{2,1,0:T(8,128)(2,1)S(1)}, bf16[4,288,128]{2,1,0:T(8,128)(2,1)}, u32[]{:S(2)}, u32[]{:S(2)}) collective-permute-start(bf16[4,288,128]{2,1,0:T(8,128)(2,1)S(1)} %rest.1.refs_2_), channel_id=1, source_target_pairs={{0,2},{2,4},{4,6},{6,0},{1,3},{3,5},{5,7},{7,1},{8,10},{10,12},{12... | collective-permute-start | bytes 884744 | tf_op jit(solution)/shard_map/ppermute | solution.py:27
  65.4 15.4 %collective-permute-start.38 = (bf16[144,1152]{1,0:T(8,128)(2,1)}, bf16[144,1152]{1,0:T(8,128)(2,1)S(1)}, u32[]{:S(2)}, u32[]{:S(2)}) collective-permute-start(bf16[144,1152]{1,0:T(8,128)(2,1)} %collective-permute-done.25.refs_20_), channel_id=1, source_target_pairs={{0,1},{1,0},{2,3},{3,2},{4,5},{5,4},{6,7},{7,6},{8,9},{9,8},{10,11... | collective-permute-start | bytes 995336 | tf_op jit(solution)/shard_map/ppermute | solution.py:27
  72.1 5.0 %copy-start.3 = (bf16[144,1152]{1,0:T(8,128)(2,1)}, bf16[144,1152]{1,0:T(8,128)(2,1)S(1)}, u32[]{:S(2)}) copy-start(bf16[144,1152]{1,0:T(8,128)(2,1)S(1)} %collective-permute-done.28.refs_22_) | copy-start | bytes 995332
  72.1 17.2 %collective-permute-start.33 = (bf16[144,1152]{1,0:T(8,128)(2,1)}, bf16[144,1152]{1,0:T(8,128)(2,1)}, u32[]{:S(2)}, u32[]{:S(2)}) collective-permute-start(bf16[144,1152]{1,0:T(8,128)(2,1)} %collective-permute-done.25.refs_20_), channel_id=1, source_target_pairs={{0,192},{64,0},{128,64},{192,128},{1,193},{65,1},{129,65},{193,129... | collective-permute-start | bytes 995336 | tf_op jit(solution)/shard_map/ppermute | solution.py:27
  73.2 1.2 copy-start.7
  73.2 16.5 %collective-permute-start.36 = (bf16[144,1152]{1,0:T(8,128)(2,1)S(1)}, bf16[144,1152]{1,0:T(8,128)(2,1)}, u32[]{:S(2)}, u32[]{:S(2)}) collective-permute-start(bf16[144,1152]{1,0:T(8,128)(2,1)S(1)} %in_order.1.refs_18_), channel_id=1, source_target_pairs={{0,1},{1,0},{2,3},{3,2},{4,5},{5,4},{6,7},{7,6},{8,9},{9,8},{10,11... | collective-permute-start | bytes 995336 | tf_op jit(solution)/shard_map/ppermute | solution.py:27
  75.3 31.5 %collective-permute-start.30 = (bf16[2,144,1152]{2,1,0:T(8,128)(2,1)S(1)}, bf16[2,144,1152]{2,1,0:T(8,128)(2,1)S(1)}, u32[]{:S(2)}, u32[]{:S(2)}) collective-permute-start(bf16[2,144,1152]{2,1,0:T(8,128)(2,1)S(1)} %pack.1.refs_21_), channel_id=1, source_target_pairs={{0,192},{64,0},{128,64},{192,128},{1,193},{65,1},{129,65},{193,129... | collective-permute-start | bytes 1990664 | tf_op jit(solution)/shard_map/ppermute | solution.py:27
  79.4 27.4 %collective-permute-start.29 = (bf16[2,144,1152]{2,1,0:T(8,128)(2,1)S(1)}, bf16[2,144,1152]{2,1,0:T(8,128)(2,1)S(1)}, u32[]{:S(2)}, u32[]{:S(2)}) collective-permute-start(bf16[2,144,1152]{2,1,0:T(8,128)(2,1)S(1)} %pack.1.refs_21_), channel_id=1, source_target_pairs={{0,64},{64,128},{128,192},{192,0},{1,65},{65,129},{129,193},{193,1... | collective-permute-start | bytes 1990664 | tf_op jit(solution)/shard_map/ppermute | solution.py:27
  80.8 0.7 copy-start.5
  81.5 18.9 %collective-permute-start.37 = (bf16[144,1152]{1,0:T(8,128)(2,1)}, bf16[144,1152]{1,0:T(8,128)(2,1)}, u32[]{:S(2)}, u32[]{:S(2)}) collective-permute-start(bf16[144,1152]{1,0:T(8,128)(2,1)} %copy-done.1), channel_id=1, source_target_pairs={{0,1},{1,0},{2,3},{3,2},{4,5},{5,4},{6,7},{7,6},{8,9},{9,8},{10,11... | collective-permute-start | bytes 995336 | tf_op jit(solution)/shard_map/ppermute | solution.py:27
  81.5 18.8 %all-to-all-start.1 = ((bf16[32,18,128]{2,1,0:T(8,128)(2,1)}), bf16[32,18,128]{2,1,0:T(8,128)(2,1)S(1)}, u32[]{:S(2)}, u32[]{:S(2)}) async-start(bf16[32,18,128]{2,1,0:T(8,128)(2,1)} %exclusive_scan.1), calls=%async_computation.1 | async-start | bytes 393216 | tf_op jit(solution)/shard_map/all_to_all | solution.py:442
  89.3 15.5 %collective-permute-start.32 = (bf16[144,1152]{1,0:T(8,128)(2,1)}, bf16[144,1152]{1,0:T(8,128)(2,1)}, u32[]{:S(2)}, u32[]{:S(2)}) collective-permute-start(bf16[144,1152]{1,0:T(8,128)(2,1)} %copy-done.3), channel_id=1, source_target_pairs={{0,192},{64,0},{128,64},{192,128},{1,193},{65,1},{129,65},{193,129... | collective-permute-start | bytes 995336 | tf_op jit(solution)/shard_map/ppermute | solution.py:27
  89.6 15.9 %collective-permute-start.31 = (bf16[144,1152]{1,0:T(8,128)(2,1)}, bf16[144,1152]{1,0:T(8,128)(2,1)}, u32[]{:S(2)}, u32[]{:S(2)}) collective-permute-start(bf16[144,1152]{1,0:T(8,128)(2,1)} %copy-done.3), channel_id=1, source_target_pairs={{0,64},{64,128},{128,192},{192,0},{1,65},{65,129},{129,193},{193,1... | collective-permute-start | bytes 995336 | tf_op jit(solution)/shard_map/ppermute | solution.py:27
  100.4 7.7 %collective-permute-start.19 = (bf16[2,288,128]{2,1,0:T(8,128)(2,1)S(1)}, bf16[2,288,128]{2,1,0:T(8,128)(2,1)S(1)}, u32[]{:S(2)}, u32[]{:S(2)}) collective-permute-start(bf16[2,288,128]{2,1,0:T(8,128)(2,1)S(1)} %join.1.refs_10_), channel_id=1, source_target_pairs={{0,1},{1,0},{2,3},{3,2},{4,5},{5,4},{6,7},{7,6},{8,9},{9,8},{10,11... | collective-permute-start | bytes 442376 | tf_op jit(solution)/shard_map/ppermute | solution.py:27
  104.8 12.6 %collective-permute-start.12 = (bf16[4,288,128]{2,1,0:T(8,128)(2,1)S(1)}, bf16[4,288,128]{2,1,0:T(8,128)(2,1)}, u32[]{:S(2)}, u32[]{:S(2)}) collective-permute-start(bf16[4,288,128]{2,1,0:T(8,128)(2,1)S(1)} %rest.1.refs_2_), channel_id=1, source_target_pairs={{0,1},{1,0},{2,3},{3,2},{4,5},{5,4},{6,7},{7,6},{8,9},{9,8},{10,11... | collective-permute-start | bytes 884744 | tf_op jit(solution)/shard_map/ppermute | solution.py:27
  105.5 8.3 %collective-permute-start.18 = (bf16[2,288,128]{2,1,0:T(8,128)(2,1)S(1)}, bf16[2,288,128]{2,1,0:T(8,128)(2,1)S(1)}, u32[]{:S(2)}, u32[]{:S(2)}) collective-permute-start(bf16[2,288,128]{2,1,0:T(8,128)(2,1)S(1)} %join.1.refs_10_), channel_id=1, source_target_pairs={{0,6},{2,0},{4,2},{6,4},{1,7},{3,1},{5,3},{7,5},{8,14},{10,8},{12,... | collective-permute-start | bytes 442376 | tf_op jit(solution)/shard_map/ppermute | solution.py:27
  106.8 8.3 %collective-permute-start.17 = (bf16[2,288,128]{2,1,0:T(8,128)(2,1)S(1)}, bf16[2,288,128]{2,1,0:T(8,128)(2,1)S(1)}, u32[]{:S(2)}, u32[]{:S(2)}) collective-permute-start(bf16[2,288,128]{2,1,0:T(8,128)(2,1)S(1)} %join.1.refs_10_), channel_id=1, source_target_pairs={{0,4},{2,6},{4,0},{6,2},{1,5},{3,7},{5,1},{7,3},{8,12},{10,14},{12... | collective-permute-start | bytes 442376 | tf_op jit(solution)/shard_map/ppermute | solution.py:27
  106.8 10.5 %collective-permute-start.16 = (bf16[2,288,128]{2,1,0:T(8,128)(2,1)S(1)}, bf16[2,288,128]{2,1,0:T(8,128)(2,1)}, u32[]{:S(2)}, u32[]{:S(2)}) collective-permute-start(bf16[2,288,128]{2,1,0:T(8,128)(2,1)S(1)} %join.1.refs_10_), channel_id=1, source_target_pairs={{0,2},{2,4},{4,6},{6,0},{1,3},{3,5},{5,7},{7,1},{8,10},{10,12},{12... | collective-permute-start | bytes 442376 | tf_op jit(solution)/shard_map/ppermute | solution.py:27
  108.1 11.1 %collective-permute-start.15 = (bf16[4,288,128]{2,1,0:T(8,128)(2,1)}, bf16[4,288,128]{2,1,0:T(8,128)(2,1)}, u32[]{:S(2)}, u32[]{:S(2)}) collective-permute-start(bf16[4,288,128]{2,1,0:T(8,128)(2,1)} %copy-done.7), channel_id=1, source_target_pairs={{0,1},{1,0},{2,3},{3,2},{4,5},{5,4},{6,7},{7,6},{8,9},{9,8},{10,11... | collective-permute-start | bytes 884744 | tf_op jit(solution)/shard_map/ppermute | solution.py:27
  113.8 4.2 %collective-permute-start.22 = (bf16[2,288,128]{2,1,0:T(8,128)(2,1)S(1)}, bf16[2,288,128]{2,1,0:T(8,128)(2,1)}, u32[]{:S(2)}, u32[]{:S(2)}) collective-permute-start(bf16[2,288,128]{2,1,0:T(8,128)(2,1)S(1)} %collective-permute-done.18.refs_13_), channel_id=1, source_target_pairs={{0,1},{1,0},{2,3},{3,2},{4,5},{5,4},{6,7},{7,6},{8,9},{9,8},{10,11... | collective-permute-start | bytes 442376 | tf_op jit(solution)/shard_map/ppermute | solution.py:27
  115.1 3.0 %collective-permute-start.21 = (bf16[2,288,128]{2,1,0:T(8,128)(2,1)S(1)}, bf16[2,288,128]{2,1,0:T(8,128)(2,1)}, u32[]{:S(2)}, u32[]{:S(2)}) collective-permute-start(bf16[2,288,128]{2,1,0:T(8,128)(2,1)S(1)} %collective-permute-done.17.refs_12_), channel_id=1, source_target_pairs={{0,1},{1,0},{2,3},{3,2},{4,5},{5,4},{6,7},{7,6},{8,9},{9,8},{10,11... | collective-permute-start | bytes 442376 | tf_op jit(solution)/shard_map/ppermute | solution.py:27
  117.3 1.7 collective-permute-start.20
  117.3 34.3 %copy-start.2 = (bf16[144,1152]{1,0:T(8,128)(2,1)S(1)}, bf16[144,1152]{1,0:T(8,128)(2,1)}, u32[]{:S(2)}) copy-start(bf16[144,1152]{1,0:T(8,128)(2,1)} %copy-done.1) | copy-start | bytes 995332
  117.3 34.3 %copy-start.4 = (bf16[144,1152]{1,0:T(8,128)(2,1)S(1)}, bf16[144,1152]{1,0:T(8,128)(2,1)}, u32[]{:S(2)}) copy-start(bf16[144,1152]{1,0:T(8,128)(2,1)} %copy-done.3) | copy-start | bytes 995332
  117.4 34.3 %copy-start.6 = (bf16[144,1152]{1,0:T(8,128)(2,1)S(1)}, bf16[144,1152]{1,0:T(8,128)(2,1)}, u32[]{:S(2)}) copy-start(bf16[144,1152]{1,0:T(8,128)(2,1)} %copy-done.5) | copy-start | bytes 995332
  117.4 34.3 %copy-start.8 = (bf16[4,288,128]{2,1,0:T(8,128)(2,1)S(1)}, bf16[4,288,128]{2,1,0:T(8,128)(2,1)}, u32[]{:S(2)}) copy-start(bf16[4,288,128]{2,1,0:T(8,128)(2,1)} %copy-done.7) | copy-start | bytes 884740
  117.4 34.3 %copy-start.9 = (f32[3,2240]{1,0:T(4,128)S(1)}, f32[3,2240]{1,0:T(4,128)}, u32[]{:S(2)}) copy-start(f32[3,2240]{1,0:T(4,128)} %refs_42_.1) | copy-start | bytes 80644
  117.4 22.1 %collective-permute-start.39 = (bf16[2,144,1152]{2,1,0:T(8,128)(2,1)S(1)}, bf16[2,144,1152]{2,1,0:T(8,128)(2,1)S(1)}, u32[]{:S(2)}, u32[]{:S(2)}) collective-permute-start(bf16[2,144,1152]{2,1,0:T(8,128)(2,1)S(1)} %pack.1.refs_21_), channel_id=1, source_target_pairs={{0,1},{1,0},{2,3},{3,2},{4,5},{5,4},{6,7},{7,6},{8,9},{9,8},{10,11... | collective-permute-start | bytes 1990664 | tf_op jit(solution)/shard_map/ppermute | solution.py:27
  118.0 4.4 %collective-permute-start.40 = (bf16[144,1152]{1,0:T(8,128)(2,1)}, bf16[144,1152]{1,0:T(8,128)(2,1)S(1)}, u32[]{:S(2)}, u32[]{:S(2)}) collective-permute-start(bf16[144,1152]{1,0:T(8,128)(2,1)} %copy-done.3), channel_id=1, source_target_pairs={{0,1},{1,0},{2,3},{3,2},{4,5},{5,4},{6,7},{7,6},{8,9},{9,8},{10,11... | collective-permute-start | bytes 995336 | tf_op jit(solution)/shard_map/ppermute | solution.py:27
  118.1 4.0 %collective-permute-start.14 = (bf16[4,288,128]{2,1,0:T(8,128)(2,1)}, bf16[4,288,128]{2,1,0:T(8,128)(2,1)S(1)}, u32[]{:S(2)}, u32[]{:S(2)}) collective-permute-start(bf16[4,288,128]{2,1,0:T(8,128)(2,1)} %collective-permute-done.10.refs_4_), channel_id=1, source_target_pairs={{0,1},{1,0},{2,3},{3,2},{4,5},{5,4},{6,7},{7,6},{8,9},{9,8},{10,11... | collective-permute-start | bytes 884744 | tf_op jit(solution)/shard_map/ppermute | solution.py:27
  119.1 3.2 %collective-permute-start.13 = (bf16[4,288,128]{2,1,0:T(8,128)(2,1)}, bf16[4,288,128]{2,1,0:T(8,128)(2,1)S(1)}, u32[]{:S(2)}, u32[]{:S(2)}) collective-permute-start(bf16[4,288,128]{2,1,0:T(8,128)(2,1)} %collective-permute-done.9.refs_3_), channel_id=1, source_target_pairs={{0,1},{1,0},{2,3},{3,2},{4,5},{5,4},{6,7},{7,6},{8,9},{9,8},{10,11... | collective-permute-start | bytes 884744 | tf_op jit(solution)/shard_map/ppermute | solution.py:27
  119.2 17.2 %collective-permute-start.34 = (bf16[2,144,1152]{2,1,0:T(8,128)(2,1)S(1)}, bf16[2,144,1152]{2,1,0:T(8,128)(2,1)S(1)}, u32[]{:S(2)}, u32[]{:S(2)}) collective-permute-start(bf16[2,144,1152]{2,1,0:T(8,128)(2,1)S(1)} %collective-permute-done.29.refs_23_), channel_id=1, source_target_pairs={{0,64},{64,128},{128,192},{192,0},{1,65},{65,129},{129,193},{193,1... | collective-permute-start | bytes 1990664 | tf_op jit(solution)/shard_map/ppermute | solution.py:27
  122.1 28.5 %collective-permute-start.5 = (bf16[2,2240,128]{2,1,0:T(8,128)(2,1)S(1)}, bf16[2,2240,128]{2,1,0:T(8,128)(2,1)S(1)}, u32[]{:S(2)}, u32[]{:S(2)}) collective-permute-start(bf16[2,2240,128]{2,1,0:T(8,128)(2,1)S(1)} %broadcast_select_fusion), channel_id=1, source_target_pairs={{0,8},{8,16},{16,24},{24,32},{32,40},{40,48},{48,56},{56,0},{1,9},... | collective-permute-start | bytes 3440648 | tf_op jit(solution)/shard_map/ppermute | solution.py:27
  122.2 17.2 %collective-permute-start.45 = (bf16[144,1152]{1,0:T(8,128)(2,1)}, bf16[144,1152]{1,0:T(8,128)(2,1)S(1)}, u32[]{:S(2)}, u32[]{:S(2)}) collective-permute-start(bf16[144,1152]{1,0:T(8,128)(2,1)} %collective-permute-done.33.refs_27_), channel_id=1, source_target_pairs={{0,1},{1,0},{2,3},{3,2},{4,5},{5,4},{6,7},{7,6},{8,9},{9,8},{10,11... | collective-permute-start | bytes 995336 | tf_op jit(solution)/shard_map/ppermute | solution.py:27
  122.4 17.6 %collective-permute-start.44 = (bf16[144,1152]{1,0:T(8,128)(2,1)}, bf16[144,1152]{1,0:T(8,128)(2,1)S(1)}, u32[]{:S(2)}, u32[]{:S(2)}) collective-permute-start(bf16[144,1152]{1,0:T(8,128)(2,1)} %collective-permute-done.32.refs_26_), channel_id=1, source_target_pairs={{0,1},{1,0},{2,3},{3,2},{4,5},{5,4},{6,7},{7,6},{8,9},{9,8},{10,11... | collective-permute-start | bytes 995336 | tf_op jit(solution)/shard_map/ppermute | solution.py:27
  136.4 10.4 %collective-permute-start.35 = (bf16[144,1152]{1,0:T(8,128)(2,1)}, bf16[144,1152]{1,0:T(8,128)(2,1)S(1)}, u32[]{:S(2)}, u32[]{:S(2)}) collective-permute-start(bf16[144,1152]{1,0:T(8,128)(2,1)} %collective-permute-done.32.refs_26_), channel_id=1, source_target_pairs={{0,192},{64,0},{128,64},{192,128},{1,193},{65,1},{129,65},{193,129... | collective-permute-start | bytes 995336 | tf_op jit(solution)/shard_map/ppermute | solution.py:27
  139.5 7.3 %collective-permute-start.43 = (bf16[144,1152]{1,0:T(8,128)(2,1)}, bf16[144,1152]{1,0:T(8,128)(2,1)S(1)}, u32[]{:S(2)}, u32[]{:S(2)}) collective-permute-start(bf16[144,1152]{1,0:T(8,128)(2,1)} %collective-permute-done.31.refs_25_), channel_id=1, source_target_pairs={{0,1},{1,0},{2,3},{3,2},{4,5},{5,4},{6,7},{7,6},{8,9},{9,8},{10,11... | collective-permute-start | bytes 995336 | tf_op jit(solution)/shard_map/ppermute | solution.py:27
  139.5 9.9 %collective-permute-start.42 = (bf16[2,144,1152]{2,1,0:T(8,128)(2,1)S(1)}, bf16[2,144,1152]{2,1,0:T(8,128)(2,1)S(1)}, u32[]{:S(2)}, u32[]{:S(2)}) collective-permute-start(bf16[2,144,1152]{2,1,0:T(8,128)(2,1)S(1)} %collective-permute-done.30.refs_24_), channel_id=1, source_target_pairs={{0,1},{1,0},{2,3},{3,2},{4,5},{5,4},{6,7},{7,6},{8,9},{9,8},{10,11... | collective-permute-start | bytes 1990664 | tf_op jit(solution)/shard_map/ppermute | solution.py:27
  140.0 9.4 %collective-permute-start.41 = (bf16[2,144,1152]{2,1,0:T(8,128)(2,1)S(1)}, bf16[2,144,1152]{2,1,0:T(8,128)(2,1)S(1)}, u32[]{:S(2)}, u32[]{:S(2)}) collective-permute-start(bf16[2,144,1152]{2,1,0:T(8,128)(2,1)S(1)} %collective-permute-done.29.refs_23_), channel_id=1, source_target_pairs={{0,1},{1,0},{2,3},{3,2},{4,5},{5,4},{6,7},{7,6},{8,9},{9,8},{10,11... | collective-permute-start | bytes 1990664 | tf_op jit(solution)/shard_map/ppermute | solution.py:27
  146.8 3.9 %collective-permute-start.46 = (bf16[2,144,1152]{2,1,0:T(8,128)(2,1)S(1)}, bf16[2,144,1152]{2,1,0:T(8,128)(2,1)S(1)}, u32[]{:S(2)}, u32[]{:S(2)}) collective-permute-start(bf16[2,144,1152]{2,1,0:T(8,128)(2,1)S(1)} %collective-permute-done.34.refs_28_), channel_id=1, source_target_pairs={{0,1},{1,0},{2,3},{3,2},{4,5},{5,4},{6,7},{7,6},{8,9},{9,8},{10,11... | collective-permute-start | bytes 1990664 | tf_op jit(solution)/shard_map/ppermute | solution.py:27
  146.8 2.6 %collective-permute-start.47 = (bf16[144,1152]{1,0:T(8,128)(2,1)S(1)}, bf16[144,1152]{1,0:T(8,128)(2,1)S(1)}, u32[]{:S(2)}, u32[]{:S(2)}) collective-permute-start(bf16[144,1152]{1,0:T(8,128)(2,1)S(1)} %collective-permute-done.35.refs_29_), channel_id=1, source_target_pairs={{0,1},{1,0},{2,3},{3,2},{4,5},{5,4},{6,7},{7,6},{8,9},{9,8},{10,11... | collective-permute-start | bytes 995336 | tf_op jit(solution)/shard_map/ppermute | solution.py:27
  150.7 1.0 copy-start.11
